TPU v7x, 32 devices: a whole 2x2x4 slice. The times are simulated.
32 devices in a mesh: gx: 4 (over x, core), gy: 8 (over z, y).
Axes of the slice: x: 2, y: 2, z: 4, core: 2. Of those that a mesh axis runs over, the one named last changes fastest.
Arguments:
- fields: float32 [4, 64, 128, 128], P(None, 'gx', 'gy'), may hold values from -6 to 6
- lift: float32 [32, 4], replicated, may hold values from -3 to 3
- lift_bias: float32 [32], replicated, may hold values from -3 to 3
- spectral_in: float32 [256, 2, 8, 32, 64], P(('gx', 'gy')), may hold values from -0.03125 to 0.03125
- bypass_in: float32 [64, 32], replicated, may hold values from -1 to 1
- bias_in: float32 [64], replicated, may hold values from -3 to 3
- spectral_out: float32 [256, 2, 8, 64, 32], P(('gx', 'gy')), may hold values from -0.046875 to 0.046875
- bypass_out: float32 [32, 64], replicated, may hold values from -0.75 to 0.75
- bias_out: float32 [32], replicated, may hold values from -3 to 3
- project: float32 [4, 32], replicated, may hold values from -1 to 1
- project_bias: float32 [4], replicated, may hold values from -3 to 3
Outputs:
- result: float32 [4, 64, 128, 128], P(None, 'gx', 'gy')
All inputs are finite; a program needn't handle non-finite values.
Results may differ from a plain program's by a relative error of at most 0.000058.
Values sent between devices are 32-bit elements; how exact they have to be, the bound alone decides.
A program may use at most 64 MiB of HBM per device.

v0:
```python
import functools
import math

import jax
import jax.numpy as jnp
import numpy as np
from jax import lax
from jax.experimental import pallas as pl
from jax.experimental.pallas import tpu as pltpu
from jax.sharding import PartitionSpec as P

KX = 16
KY = 16
KZ = 8
YB = 8
LB = 128
GROUP = 4
F32 = jnp.float32
BF16 = jnp.bfloat16
MESH = pl.DeviceIdType.MESH


def freq(count):
    f = np.arange(count)
    return np.where(f < count // 2, f, f - count)


def halves(table):
    high = table.astype(np.float32).astype(jnp.bfloat16)
    low = (table - high.astype(np.float64)).astype(np.float32).astype(jnp.bfloat16)
    return np.stack([high, low])


def stacked(table):
    high, low = halves(table)
    return np.concatenate([high, high, low], axis=0)


def angles(places, frequency, length):
    turns = np.mod(places[:, None] * frequency[None, :], length)
    return turns * (2.0 * math.pi / length)


def z_table(z_length):
    ang = angles(np.arange(z_length), np.arange(KZ), z_length)
    table = np.zeros((YB, z_length, 2, YB, KZ))
    for y in range(YB):
        table[y, :, 0, y] = np.cos(ang)
        table[y, :, 1, y] = -np.sin(ang)
    return table.reshape(YB * z_length, LB)


def y_table(blocks, cells, length, groups):
    per = KY // groups
    frequency = freq(KY)
    out = np.zeros((blocks, cells // YB, 2, YB, KZ, groups, LB))
    for b in range(blocks):
        ang = angles(b * cells + np.arange(cells), frequency, length)
        for y in range(cells):
            for j in range(KY):
                c, s = np.cos(ang[y, j]), np.sin(ang[y, j])
                for k in range(KZ):
                    re = (j % per) * KZ + k
                    im = per * KZ + re
                    at = (b, y // YB)
                    out[at + (0, y % YB, k, j // per, re)] = c
                    out[at + (1, y % YB, k, j // per, re)] = s
                    out[at + (0, y % YB, k, j // per, im)] = -s
                    out[at + (1, y % YB, k, j // per, im)] = c
    return out.reshape(blocks, cells // YB * LB, groups * LB)


def x_angles(blocks, cells, length):
    return angles(np.arange(blocks * cells), freq(KX), length).reshape(blocks, cells, KX)


def split(value):
    high = value.astype(BF16)
    return high, (value - high.astype(F32)).astype(BF16)


def mul(a, b):
    return jnp.dot(a, b, preferred_element_type=F32)


def tall(a):
    return jnp.concatenate([a[0], a[1], a[0]], axis=1)


def deep(a):
    return jnp.concatenate([a[0], a[1], a[0]], axis=0)


def wide(a):
    return jnp.concatenate([a[0], a[0], a[1]], axis=1)


def mul3(a, b):
    return mul(a[0], b[0]) + (mul(a[1], b[0]) + mul(a[0], b[1]))


def gelu(v):
    return (0.5 * v) * (1.0 + lax.erf(v * math.sqrt(0.5)))


def kernel(
    A, B, cells_x, scale1, scale2, gain,
    f_ref, lift_ref, lbias_ref, byp_ref, bi_ref, wo_ref, bo_ref, pr_ref, pb_ref,
    tzf_ref, cs_ref, tzi_hbm, w1_hbm, w2_hbm, tx_hbm, yf1_hbm, yfc_hbm, yic_hbm, yi2_hbm,
    o_ref,
    tzi_ref, w1, w2, tx, yf1, yfc, yic, yi2,
    buf1, r1, mx, mt1, ag1, yb1, ya1, zc, fx2, r2, buf2, r3, mt2, ag2, yb2, ya2, nar, yr1, yr2, pk_ref, fk_ref, t16, bd,
    csem, ssem, rsem,
):
    a = lax.axis_index("gx")
    b = lax.axis_index("gy")
    me = a * B + b
    IL = KX // A
    H = B // IL
    J = KY // H
    N = A * B
    CIN, C1 = lift_ref.shape
    C2 = wo_ref.shape[1]
    hx = cells_x // 2

    loads = [
        pltpu.make_async_copy(tx_hbm.at[a], tx, csem.at[0]),
        pltpu.make_async_copy(yf1_hbm.at[b], yf1, csem.at[1]),
        pltpu.make_async_copy(w1_hbm, w1, csem.at[2]),
        pltpu.make_async_copy(yic_hbm.at[b], yic, csem.at[3]),
        pltpu.make_async_copy(yfc_hbm.at[b], yfc, csem.at[4]),
        pltpu.make_async_copy(w2_hbm, w2, csem.at[5]),
        pltpu.make_async_copy(yi2_hbm.at[b], yi2, csem.at[6]),
        pltpu.make_async_copy(tzi_hbm, tzi_ref, csem.at[7]),
    ]
    for load in loads:
        load.start()

    barrier = pltpu.get_barrier_semaphore()
    for step in range(1, N):
        peer = lax.rem(me + step, N)
        pl.semaphore_signal(
            barrier, inc=1, device_id=(peer // B, lax.rem(peer, B)), device_id_type=MESH
        )

    lane = lax.broadcasted_iota(jnp.int32, (1, LB), 1)
    sign_f = jnp.where(lane < LB // 2, 1.0, -1.0).astype(F32)

    def rot_f(v):
        return pltpu.roll(v, LB // 2, 1) * sign_f

    def rot_i(v):
        return pltpu.roll(v, LB // 2, 1) * -sign_f

    width = tzi_ref.shape[1]
    zs = []
    for ch in range(2):
        zs.append(mul(tall(split(f_ref[:, ch * width:(ch + 1) * width])), tzf_ref[...]))
    loads[0].wait()
    us = []
    for z in zs:
        us.append(mul3((tx[0], tx[1]), split(jnp.concatenate([z, rot_f(z)], axis=0))))
    loads[1].wait()
    part = mul3(split(jnp.concatenate(us, axis=1)), (yf1[0], yf1[1]))
    for i in range(KX):
        for h in range(H):
            buf1[i * H + h] = part[i * CIN:(i + 1) * CIN, h * LB:(h + 1) * LB]
    r1[me] = buf1[me]
    pl.semaphore_wait(barrier, N - 1)

    sends = []
    phase = []
    for step in range(1, N):
        peer = lax.rem(me + step, N)
        phase.append(pltpu.make_async_remote_copy(
            src_ref=buf1.at[peer], dst_ref=r1.at[me], send_sem=ssem.at[peer], recv_sem=rsem.at[me],
            device_id=(peer // B, lax.rem(peer, B)), device_id_type=MESH,
        ))
    for copy in phase:
        copy.start()
    sends += phase
    loads[2].wait()
    mx[...] = jnp.zeros_like(mx)
    mx[0:CIN, :C1] = lift_ref[...]
    mx[CIN:CIN + 1, :C1] = lbias_ref[...]
    mx[CIN + 1:CIN + 2, :C1] = bo_ref[...]
    lift8 = jnp.concatenate([mx[0:8, :C1]], axis=0)
    columns = mx[...].T[:C1]
    bo_col = columns[:, CIN + 1:CIN + 2]

    def left16(matrix, bias):
        n = matrix.shape[1]
        high, low = split(matrix[0:CIN])
        b0 = bias.astype(BF16)
        rest = bias - b0.astype(F32)
        b1 = rest.astype(BF16)
        b2 = (rest - b1.astype(F32)).astype(BF16)
        mx[...] = jnp.zeros_like(mx)
        mx[0:CIN, :n] = high.astype(F32)
        mx[CIN:2 * CIN, :n] = high.astype(F32)
        mx[2 * CIN:3 * CIN, :n] = low.astype(F32)
        for row, value in enumerate((b0, b1, b2)):
            mx[3 * CIN + row:3 * CIN + row + 1, :n] = value.astype(F32)
        return mx[...].T[:n, :16].astype(BF16)

    highest = lax.Precision.HIGHEST
    m = jnp.dot(lift8, byp_ref[...], precision=highest, preferred_element_type=F32)
    bp16 = left16(m, m[CIN:CIN + 1] + bi_ref[...])
    m = lax.dot_general(
        lift8, pr_ref[...], (((1,), (1,)), ((), ())), precision=highest, preferred_element_type=F32
    )
    pl16 = left16(m, m[CIN:CIN + 1] + pb_ref[...])
    t16[...] = jnp.ones_like(t16)

    def diagonal(value):
        rows, cols = value.shape
        bd[...] = jnp.zeros_like(bd)
        for g in range(GROUP):
            bd[g * rows:(g + 1) * rows, g * cols:(g + 1) * cols] = value
        return bd[0:GROUP * rows, 0:GROUP * cols]

    bp_bd = diagonal(bp16.astype(F32)).astype(BF16)
    pl_bd = diagonal(pl16.astype(F32)).astype(BF16)
    wo_bd = wide(split(diagonal(wo_ref[...])))
    pr_bd = wide(split(diagonal(pr_ref[...])))
    for step in range(1, N):
        peer = lax.rem(me + step, N)
        pltpu.make_async_remote_copy(
            src_ref=buf1.at[peer], dst_ref=r1.at[peer], send_sem=ssem.at[peer], recv_sem=rsem.at[peer],
            device_id=(peer // B, lax.rem(peer, B)), device_id_type=MESH,
        ).wait_recv()

    own = b // H
    gy_slot = [N, N + B, N + 2 * B]
    gx_slot = [N + 3 * B, N + 3 * B + KX, N + 3 * B + 2 * KX]

    def to_gy(source, target, slot, peer, index):
        return pltpu.make_async_remote_copy(
            src_ref=source, dst_ref=target.at[index], send_sem=ssem.at[gy_slot[slot] + peer],
            recv_sem=rsem.at[gy_slot[slot] + index], device_id=(a, peer), device_id_type=MESH,
        )

    def to_gx(source, target, slot, peer, index, il):
        return pltpu.make_async_remote_copy(
            src_ref=source, dst_ref=target.at[index, il],
            send_sem=ssem.at[gx_slot[slot] + peer * IL + il],
            recv_sem=rsem.at[gx_slot[slot] + index * IL + il],
            device_id=(peer, b), device_id_type=MESH,
        )

    def send(copy):
        copy.start()
        sends.append(copy)

    def gather(block, ag, slot):
        for step in range(1, B):
            peer = lax.rem(b + step, B)
            send(to_gy(block, ag, slot, peer, b))

    def expand(block, ag, table, yb, ya, slot, gx):
        for s in range(IL):
            il = lax.rem(own + s, IL)
            for t in range(1 if s == 0 else 0, H):
                source = il * H + lax.rem(b + t, H)
                to_gy(block, ag, slot, source, source).wait_recv()
            rows = jnp.concatenate([ag[il * H + h] for h in range(H)], axis=1)
            y = mul3(split(rows), (table[0], table[1]))
            yb[il] = y
            ya[a, il] = y
            for step in range(1, A):
                peer = lax.rem(a + step, A)
                send(to_gx(yb.at[il], ya, gx, peer, a, il))
        for s in range(IL):
            il = lax.rem(own + s, IL)
            for step in range(1, A):
                peer = lax.rem(a + step, A)
                to_gx(yb.at[il], ya, gx, peer, peer, il).wait_recv()

    def mix(st, w, width_out):
        mx[...] = jnp.zeros_like(mx)
        for j in range(J):
            for k in range(KZ):
                q = j * KZ + k
                p = J * KZ + q
                re = st[:, q:q + 1]
                im = st[:, p:p + 1]
                wr = w[j, 0, k]
                wi = w[j, 1, k]
                mx[q:q + 1, :width_out] = jnp.sum(re * wr - im * wi, axis=0, keepdims=True)
                mx[p:p + 1, :width_out] = jnp.sum(re * wi + im * wr, axis=0, keepdims=True)
        return mx[...].T[:width_out]

    s4 = jnp.sum(r1[...], axis=0) * scale1
    st = columns[:, 0:1] * s4[0:1]
    for c in range(1, CIN):
        st = st + columns[:, c:c + 1] * s4[c:c + 1]
    first = jnp.where((lane == 0) & (me == 0), gain, 0.0).astype(F32)
    st = st + columns[:, CIN:CIN + 1] * first
    mixed = mix(st, w1, C2)
    mt1[...] = mixed
    ag1[b] = mixed
    gather(mt1, ag1, 0)
    zn = width // YB

    def fill(value):
        n = value.shape[1]
        high, low = split(value)
        t16[0:CIN, :n] = high.astype(F32)
        t16[CIN:2 * CIN, :n] = low.astype(F32)
        t16[2 * CIN:3 * CIN, :n] = high.astype(F32)
        return t16[:, :n].astype(BF16)

    for x in range(hx):
        one = f_ref[2 * x * CIN:(2 * x + 1) * CIN]
        two = f_ref[(2 * x + 1) * CIN:(2 * x + 2) * CIN]
        fk_ref[2 * x] = fill(one)
        fk_ref[2 * x + 1] = fill(two)
        both = one + two
        pieces = [
            both[:, 2 * y * zn:(2 * y + 1) * zn] + both[:, (2 * y + 1) * zn:(2 * y + 2) * zn]
            for y in range(YB)
        ]
        pk_ref[x] = fill(jnp.concatenate(pieces, axis=1) * 0.25)
    loads[3].wait()
    expand(mt1, ag1, yic, yb1, ya1, 0, 0)
    for i in range(KX):
        yr1[i] = rot_i(ya1[i // IL, i % IL])

    HC = hx * KX

    def coarse_step(group, carry):
        parts = []
        for xx in range(GROUP):
            x = group * GROUP + xx
            acc = jnp.zeros((C2, LB), F32)
            for i in range(KX):
                c = cs_ref[a, x * KX + i]
                s = cs_ref[a, HC + x * KX + i]
                acc = acc + (c * ya1[i // IL, i % IL] + s * yr1[i])
            parts.append(acc)
        v = mul(tall(split(jnp.concatenate(parts, axis=0))), tzi_ref[...])
        near = jnp.concatenate([pk_ref[group * GROUP + xx] for xx in range(GROUP)], axis=0)
        g = split(gelu(v + mul(bp_bd, near)))
        narrow = mul(wo_bd, deep(g))
        wave = mul(tall(g), tzf_ref[...])
        for xx in range(GROUP):
            nar[group * GROUP + xx] = narrow[xx * C1:(xx + 1) * C1]
            zc[group * GROUP + xx] = wave[xx * C2:(xx + 1) * C2]
        return carry

    loads[7].wait()
    lax.fori_loop(0, hx // GROUP, coarse_step, 0)

    order = [lax.rem(own + 1 + s, IL) for s in range(IL)]
    for il in order:
        for t in range(A):
            peer = lax.rem(a + 1 + t, A)
            i = peer * IL + il
            re = jnp.zeros((C2, LB), F32)
            im = jnp.zeros((C2, LB), F32)
            for x in range(hx):
                re = re + cs_ref[a, x * KX + i] * zc[x]
                im = im + cs_ref[a, HC + x * KX + i] * zc[x]
            value = re + rot_f(im)
            if t < A - 1:
                fx2[peer, il] = value
                send(to_gx(fx2.at[peer, il], r2, 1, peer, a, il))
            else:
                r2[a, il] = value
    loads[4].wait()
    for s, il in enumerate(order):
        for step in range(1, A):
            peer = lax.rem(a + step, A)
            to_gx(fx2.at[peer, il], r2, 1, peer, peer, il).wait_recv()
        total = r2[0, il]
        for peer in range(1, A):
            total = total + r2[peer, il]
        out = mul3(split(total), (yfc[0], yfc[1]))
        for h in range(H):
            buf2[il * H + h] = out[:, h * LB:(h + 1) * LB]
        for t in range(1 if s == IL - 1 else 0, H):
            peer = il * H + lax.rem(b + t, H)
            send(to_gy(buf2.at[peer], r3, 1, peer, b))
    r3[b] = buf2[b]
    loads[5].wait()
    for step in range(1, B):
        peer = lax.rem(b + step, B)
        to_gy(buf2.at[peer], r3, 1, peer, peer).wait_recv()
    st = (jnp.sum(r3[...], axis=0) * scale2).T
    mixed = jnp.zeros((C1, LB), F32)
    for j in range(J):
        for k in range(KZ):
            q = j * KZ + k
            p = J * KZ + q
            re = st[q:q + 1]
            im = st[p:p + 1]
            wr = w2[j, 0, k]
            wi = w2[j, 1, k]
            real = jnp.sum(re * wr - im * wi, axis=1, keepdims=True)
            imag = jnp.sum(re * wi + im * wr, axis=1, keepdims=True)
            mixed = jnp.where(lane == q, real, jnp.where(lane == p, imag, mixed))
    mt2[...] = mixed
    ag2[b] = mixed
    gather(mt2, ag2, 2)
    loads[6].wait()
    expand(mt2, ag2, yi2, yb2, ya2, 2, 2)
    for i in range(KX):
        for ch in range(2):
            part = slice(ch * LB, (ch + 1) * LB)
            yr2[i, :, part] = rot_i(ya2[i // IL, i % IL, :, part])

    FC = cells_x * KX

    def fine_step(group, carry):
        parts = []
        for xx in range(GROUP):
            x = group * GROUP + xx
            acc = jnp.zeros((C1, 2 * LB), F32)
            for i in range(KX):
                c = cs_ref[a, 2 * HC + x * KX + i]
                s = cs_ref[a, 2 * HC + FC + x * KX + i]
                acc = acc + (c * ya2[i // IL, i % IL] + s * yr2[i])
            parts.append(acc)
        near = jnp.concatenate([fk_ref[group * GROUP + xx] for xx in range(GROUP)], axis=0)
        for ch in range(2):
            lines = jnp.concatenate([part[:, ch * LB:(ch + 1) * LB] for part in parts], axis=0)
            v = mul(tall(split(lines)), tzi_ref[...])
            rows = []
            for xx in range(0, GROUP, 2):
                half = nar.at[group * (GROUP // 2) + xx // 2]
                pieces = []
                for yy in range(YB):
                    at = (ch * YB + yy) // 2 * zn
                    pieces.append(half[:, at:at + zn])
                rows += [jnp.concatenate(pieces, axis=1) + bo_col] * 2
            g = split(gelu(v + jnp.concatenate(rows, axis=0)))
            cols = slice(ch * width, (ch + 1) * width)
            res = mul(pr_bd, deep(g)) + mul(pl_bd, near[:, cols])
            for xx in range(GROUP):
                o_ref[group * GROUP + xx, :, cols] = res[xx * CIN:(xx + 1) * CIN]
        return carry

    lax.fori_loop(0, cells_x // GROUP, fine_step, 0)
    for copy in sends:
        copy.wait_send()


def on_device(
    A, B, fields, lift, lift_bias, spectral_in, bypass_in, bias_in, spectral_out, bypass_out,
    bias_out, proj, proj_bias,
):
    cin, xc, yc, zc = fields.shape
    C1 = lift.shape[0]
    C2 = bypass_in.shape[0]
    NX = xc * A
    NY = yc * B
    IL = KX // A
    H = B // IL
    J = KY // H
    N = A * B
    width = YB * zc
    cells = float(NX * NY * zc)
    back = math.sqrt(2.0 / (KX * KY * KZ))

    tz = z_table(zc)
    tzf = stacked(tz)
    tzi = stacked(np.ascontiguousarray(tz.T) * back)
    fine_x = x_angles(A, xc, NX)
    half_x = x_angles(A, xc // 2, NX // 2)
    eye = np.eye(cin)
    tx = np.stack([
        np.concatenate([np.kron(np.cos(fine_x[i].T), eye), np.kron(np.sin(fine_x[i].T), eye)], axis=1)
        for i in range(A)
    ])
    cs = np.concatenate([
        np.cos(half_x).reshape(A, -1), np.sin(half_x).reshape(A, -1),
        np.cos(fine_x).reshape(A, -1), np.sin(fine_x).reshape(A, -1),
    ], axis=1).astype(np.float32)
    yf1 = y_table(B, yc, NY, H)
    yfc = y_table(B, yc // 2, NY // 2, H)

    def per_device(table):
        return jnp.asarray(np.ascontiguousarray(np.swapaxes(halves(table), 0, 1)))

    tx_t = per_device(tx)
    yf1_t = per_device(yf1)
    yfc_t = per_device(yfc)
    yic_t = per_device(np.swapaxes(yfc, 1, 2))
    yi2_t = per_device(np.swapaxes(yf1, 1, 2))

    rows = jnp.transpose(fields, (1, 0, 2, 3)).reshape(xc * cin, yc * zc)
    weights2 = jnp.swapaxes(spectral_out, 3, 4)

    vmem = pl.BlockSpec(memory_space=pltpu.VMEM)
    anywhere = pl.BlockSpec(memory_space=pl.ANY)
    V = pltpu.VMEM
    out = pl.pallas_call(
        functools.partial(
            kernel, A, B, xc, 1.0 / math.sqrt(cells), 1.0 / math.sqrt(cells / 4.0), math.sqrt(cells)
        ),
        out_shape=jax.ShapeDtypeStruct((xc, cin, yc * zc), F32),
        in_specs=[vmem] * 10 + [pl.BlockSpec(memory_space=pltpu.SMEM)] + [anywhere] * 8,
        out_specs=vmem,
        scratch_shapes=[
            V(tzi.shape, BF16), V(spectral_in.shape, F32), V(weights2.shape, F32),
            V(tx_t.shape[1:], BF16), V(yf1_t.shape[1:], BF16), V(yfc_t.shape[1:], BF16),
            V(yic_t.shape[1:], BF16), V(yi2_t.shape[1:], BF16),
            V((N, cin, LB), F32), V((N, cin, LB), F32), V((LB, LB), F32),
            V((C2, LB), F32), V((B, C2, LB), F32),
            V((IL, C2, LB), F32), V((A, IL, C2, LB), F32),
            V((xc // 2, C2, LB), F32), V((A, IL, C2, LB), F32), V((A, IL, C2, LB), F32),
            V((B, C2, LB), F32), V((B, C2, LB), F32),
            V((C1, LB), F32), V((B, C1, LB), F32),
            V((IL, C1, 2 * LB), F32), V((A, IL, C1, 2 * LB), F32),
            V((xc // 2, C1, width), F32), V((KX, C2, LB), F32), V((KX, C1, 2 * LB), F32),
            V((xc // 2, 16, width), BF16), V((xc, 16, yc * zc), BF16), V((16, yc * zc), F32), V((GROUP * C2, GROUP * C2), F32),
            pltpu.SemaphoreType.DMA((8,)),
            pltpu.SemaphoreType.DMA((N + 3 * B + 3 * KX,)), pltpu.SemaphoreType.DMA((N + 3 * B + 3 * KX,)),
        ],
        compiler_params=pltpu.CompilerParams(
            collective_id=0, has_side_effects=True, vmem_limit_bytes=60 * 1024 * 1024
        ),
    )(
        rows, lift.T, lift_bias[None], bypass_in.T, bias_in[None], bypass_out, bias_out[None], proj,
        proj_bias[None], jnp.asarray(tzf), jnp.asarray(cs),
        jnp.asarray(tzi), spectral_in, weights2, tx_t, yf1_t, yfc_t, yic_t, yi2_t,
    )
    return jnp.transpose(out.reshape(xc, cin, yc, zc), (1, 0, 2, 3))


def solution(mesh):
    A = mesh.shape["gx"]
    B = mesh.shape["gy"]
    in_specs = (
        P(None, "gx", "gy", None), P(), P(), P(("gx", "gy"), None, None, None, None), P(), P(),
        P(("gx", "gy"), None, None, None, None), P(), P(), P(), P(),
    )
    return jax.shard_map(
        functools.partial(on_device, A, B), mesh=mesh, in_specs=in_specs,
        out_specs=P(None, "gx", "gy", None), check_vma=False,
    )
```

profile of v0, /device:TPU:0, one launch (start us, length us, event | category | flops | bytes accessed | tf_op | source)
XLA Modules:
  0.0 64.5 jit_solution(11612581790981627121)
XLA Ops:
  0.0 1.1 %copy.20 = f32[16,4,16,128]{3,2,1,0:T(8,128)S(1)} copy(f32[16,4,16,128]{3,2,0,1:T(8,128)} %bitcast.19) | data formatting | bytes 1048576 | tf_op jit(solution)/shard_map/transpose | solution.py:491
  1.1 1.0 %copy.25 = f32[8,8,16,128]{3,1,2,0:T(8,128)} copy(f32[8,8,16,128]{3,2,1,0:T(8,128)S(1)} %bitcast.17) | data formatting | bytes 1048576
  2.0 60.3 %shard_map.181 = f32[16,4,2048]{2,1,0:T(4,128)} custom-call(f32[64,2048]{1,0:T(8,128)} %bitcast.16, f32[4,32]{1,0:T(4,128)} %bitcast.21, f32[1,32]{1,0:T(1,128)} %bitcast.22, f32[32,64]{1,0:T(8,128)} %bitcast.20, f32[1,64]{1,0:T(1,128)} %bitcast.23, f32[32,64]{1,0:T(8,128)} %wo_ref.1, f32[1,32]{1,0:T(1,128)} %bitcast.24, f32[4,32]{1,0:T(4,128)} %pr_ref.1, ...), custom_call_target="tpu_custom_call" | custom-call | tf_op jit(solution)/shard_map/pallas_call | solution.py:497
  62.3 1.3 %reshape.7 = f32[16,4,16,128]{3,2,1,0:T(8,128)S(1)} reshape(f32[16,4,2048]{2,1,0:T(4,128)} %shard_map.181) | data formatting | bytes 1048576 | tf_op jit(solution)/shard_map/reshape | solution.py:528
  63.6 0.8 %copy.26 = f32[16,4,16,128]{3,2,0,1:T(8,128)} copy(f32[16,4,16,128]{3,2,1,0:T(8,128)S(1)} %reshape.7) | data formatting | bytes 1048576 | tf_op jit(solution)/shard_map/reshape | solution.py:528
where the time goes:
time: 64.7 us; the launch traced here: 64.5 us
  Pallas kernels  60.3 us (93%)
  local copies, waits for them, and re-layouts  4.19 us (6%)
    pallas_call x1, Pallas kernels, on_device(): pl.pallas_call(functools.partial(kernel, A, B, xc, 1.0 / math.sqrt(cells)...  60.3 us
    reshape x2, local copies, waits for them, and re-layouts, on_device(): return jnp.transpose(out.reshape(xc, cin, yc, zc), (1, 0, 2, 3))  2.15 us

commit v1 on v0

v1 whole, which is shorter than its diff:
```python
import functools
import math

import jax
import jax.numpy as jnp
import numpy as np
from jax import lax
from jax.experimental import pallas as pl
from jax.experimental.pallas import tpu as pltpu
from jax.sharding import PartitionSpec as P

KX = 16
KY = 16
KZ = 8
YB = 8
LB = 128
GROUP = 4
F32 = jnp.float32
BF16 = jnp.bfloat16
MESH = pl.DeviceIdType.MESH


def freq(count):
    f = np.arange(count)
    return np.where(f < count // 2, f, f - count)


def halves(table):
    high = table.astype(np.float32).astype(jnp.bfloat16)
    low = (table - high.astype(np.float64)).astype(np.float32).astype(jnp.bfloat16)
    return np.stack([high, low])


def stacked(table):
    high, low = halves(table)
    return np.concatenate([high, high, low], axis=0)


def angles(places, frequency, length):
    turns = np.mod(places[:, None] * frequency[None, :], length)
    return turns * (2.0 * math.pi / length)


def z_table(z_length):
    ang = angles(np.arange(z_length), np.arange(KZ), z_length)
    table = np.zeros((YB, z_length, 2, YB, KZ))
    for y in range(YB):
        table[y, :, 0, y] = np.cos(ang)
        table[y, :, 1, y] = -np.sin(ang)
    return table.reshape(YB * z_length, LB)


def y_table(blocks, cells, length, groups):
    per = KY // groups
    frequency = freq(KY)
    out = np.zeros((blocks, cells // YB, 2, YB, KZ, groups, LB))
    for b in range(blocks):
        ang = angles(b * cells + np.arange(cells), frequency, length)
        for y in range(cells):
            for j in range(KY):
                c, s = np.cos(ang[y, j]), np.sin(ang[y, j])
                for k in range(KZ):
                    re = (j % per) * KZ + k
                    im = per * KZ + re
                    at = (b, y // YB)
                    out[at + (0, y % YB, k, j // per, re)] = c
                    out[at + (1, y % YB, k, j // per, re)] = s
                    out[at + (0, y % YB, k, j // per, im)] = -s
                    out[at + (1, y % YB, k, j // per, im)] = c
    return out.reshape(blocks, cells // YB * LB, groups * LB)


def x_angles(blocks, cells, length):
    return angles(np.arange(blocks * cells), freq(KX), length).reshape(blocks, cells, KX)


def split(value):
    high = value.astype(BF16)
    return high, (value - high.astype(F32)).astype(BF16)


def mul(a, b):
    return jnp.dot(a, b, preferred_element_type=F32)


def tall(a):
    return jnp.concatenate([a[0], a[1], a[0]], axis=1)


def deep(a):
    return jnp.concatenate([a[0], a[1], a[0]], axis=0)


def wide(a):
    return jnp.concatenate([a[0], a[0], a[1]], axis=1)


def mul3(a, b):
    return mul(a[0], b[0]) + (mul(a[1], b[0]) + mul(a[0], b[1]))


def gelu(v):
    return (0.5 * v) * (1.0 + lax.erf(v * math.sqrt(0.5)))


def kernel(
    A, B, cells_x, scale1, scale2, gain,
    f_ref, lift_ref, lbias_ref, byp_ref, bi_ref, wo_ref, bo_ref, pr_ref, pb_ref,
    tzf_ref, tzi_hbm, w1_hbm, w2_hbm, tx_hbm, yf1_hbm, yfc_hbm, yic_hbm, yi2_hbm, xf_hbm, xi_hbm, xo_hbm,
    o_ref,
    tzi_ref, w1, w2, tx, yf1, yfc, yic, yi2, xf, xi, xo,
    buf1, r1, mx, mt1, g1, yall, pg, pk_ref, vx, zc, vn, buf2, r3, ag2, vf, nar, fk_ref, t16, bd, bpq,
    csem, ssem, rsem,
):
    a = lax.axis_index("gx")
    b = lax.axis_index("gy")
    me = a * B + b
    IL = KX // A
    H = B // IL
    J = KY // H
    N = A * B
    X = A // 2
    CIN, C1 = lift_ref.shape
    C2 = wo_ref.shape[1]
    CQ = C2 // A
    CG = CQ // 8
    hx = cells_x // 2
    HX = hx * A
    G1 = GROUP * C2 // CQ
    own_g = b // H
    own_h = lax.rem(b, H)
    core = lax.rem(a, 2)
    sib = a + 1 - 2 * core
    mates = [lax.rem(a + 2 * s, A) for s in range(1, X)]

    pairs = [
        (tx_hbm.at[a], tx), (yf1_hbm.at[b], yf1), (w1_hbm, w1), (yic_hbm.at[b], yic), (xi_hbm, xi), (tzi_hbm, tzi_ref),
        (xf_hbm, xf), (yfc_hbm.at[b], yfc), (w2_hbm, w2), (yi2_hbm.at[b], yi2), (xo_hbm.at[a], xo),
    ]
    loads = [pltpu.make_async_copy(src, dst, csem.at[k]) for k, (src, dst) in enumerate(pairs)]
    l_tx, l_yf1, l_w1, l_yic, l_xi, l_tzi, l_xf, l_yfc, l_w2, l_yi2, l_xo = loads
    for load in loads:
        load.start()

    barrier = pltpu.get_barrier_semaphore()
    for step in range(1, N):
        peer = lax.rem(me + step, N)
        pl.semaphore_signal(
            barrier, inc=1, device_id=(peer // B, lax.rem(peer, B)), device_id_type=MESH
        )

    lane = lax.broadcasted_iota(jnp.int32, (1, LB), 1)
    sign_f = jnp.where(lane < LB // 2, 1.0, -1.0).astype(F32)

    def rot_f(v):
        return pltpu.roll(v, LB // 2, 1) * sign_f

    def rot_i(v):
        return pltpu.roll(v, LB // 2, 1) * -sign_f

    sends = []
    used = [0]

    def remote(source, target, slot, device):
        copy = pltpu.make_async_remote_copy(
            src_ref=source, dst_ref=target, send_sem=ssem.at[used[0]], recv_sem=rsem.at[slot],
            device_id=device, device_id_type=MESH,
        )
        used[0] += 1
        copy.start()
        sends.append(copy)

    def arrive(target, slot):
        pltpu.make_async_remote_copy(
            src_ref=target, dst_ref=target, send_sem=ssem.at[0], recv_sem=rsem.at[slot],
            device_id=(sib, b), device_id_type=MESH,
        ).wait_recv()

    def at(index):
        return (index // B, lax.rem(index, B))

    S_EXP1, S_RED, S_EXP2, S_POOL, S_Y = N, 2 * N, 3 * N, 4 * N, 4 * N + A

    width = tzi_ref.shape[1]
    zs = []
    for ch in range(2):
        zs.append(mul(tall(split(f_ref[:, ch * width:(ch + 1) * width])), tzf_ref[...]))
    l_tx.wait()
    us = []
    for z in zs:
        us.append(mul3((tx[0], tx[1]), split(jnp.concatenate([z, rot_f(z)], axis=0))))
    l_yf1.wait()
    part = mul3(split(jnp.concatenate(us, axis=1)), (yf1[0], yf1[1]))
    for i in range(KX):
        for h in range(H):
            buf1[i * H + h] = part[i * CIN:(i + 1) * CIN, h * LB:(h + 1) * LB]
    r1[me] = buf1[me]
    pl.semaphore_wait(barrier, N - 1)

    for step in range(1, N):
        peer = lax.rem(me + step, N)
        remote(buf1.at[peer], r1.at[me], me, at(peer))

    zn = width // YB
    for x in range(hx):
        both = f_ref[2 * x * CIN:(2 * x + 1) * CIN] + f_ref[(2 * x + 1) * CIN:(2 * x + 2) * CIN]
        pieces = [
            both[:, 2 * y * zn:(2 * y + 1) * zn] + both[:, (2 * y + 1) * zn:(2 * y + 2) * zn]
            for y in range(YB)
        ]
        pg[a, x * CIN:(x + 1) * CIN] = jnp.concatenate(pieces, axis=1) * 0.25

    def near_send(buffer, slot):
        for peer in mates + [sib]:
            remote(buffer.at[a], buffer.at[a], slot + a, (peer, b))

    def near_forward(buffer, slot):
        for peer in mates:
            arrive(buffer.at[peer], slot + peer)
            remote(buffer.at[peer], buffer.at[peer], slot + peer, (sib, b))

    def near_finish(buffer, slot):
        arrive(buffer.at[sib], slot + sib)
        for peer in mates:
            other = peer + 1 - 2 * core
            arrive(buffer.at[other], slot + other)

    near_send(pg, S_POOL)

    l_w1.wait()
    mx[...] = jnp.zeros_like(mx)
    mx[0:CIN, :C1] = lift_ref[...]
    mx[CIN:CIN + 1, :C1] = lbias_ref[...]
    mx[CIN + 1:CIN + 2, :C1] = bo_ref[...]
    lift8 = jnp.concatenate([mx[0:8, :C1]], axis=0)
    columns = mx[...].T[:C1]
    bo_col = columns[:, CIN + 1:CIN + 2]

    def left16(matrix, bias):
        n = matrix.shape[1]
        high, low = split(matrix[0:CIN])
        b0 = bias.astype(BF16)
        rest = bias - b0.astype(F32)
        b1 = rest.astype(BF16)
        b2 = (rest - b1.astype(F32)).astype(BF16)
        mx[...] = jnp.zeros_like(mx)
        mx[0:CIN, :n] = high.astype(F32)
        mx[CIN:2 * CIN, :n] = high.astype(F32)
        mx[2 * CIN:3 * CIN, :n] = low.astype(F32)
        for row, value in enumerate((b0, b1, b2)):
            mx[3 * CIN + row:3 * CIN + row + 1, :n] = value.astype(F32)
        return mx[...].T[:n, :16].astype(BF16)

    highest = lax.Precision.HIGHEST
    m = jnp.dot(lift8, byp_ref[...], precision=highest, preferred_element_type=F32)
    bp16 = left16(m, m[CIN:CIN + 1] + bi_ref[...])
    m = lax.dot_general(
        lift8, pr_ref[...], (((1,), (1,)), ((), ())), precision=highest, preferred_element_type=F32
    )
    pl16 = left16(m, m[CIN:CIN + 1] + pb_ref[...])
    t16[...] = jnp.ones_like(t16)

    def diagonal(value, count):
        rows, cols = value.shape
        bd[...] = jnp.zeros_like(bd)
        for g in range(count):
            bd[g * rows:(g + 1) * rows, g * cols:(g + 1) * cols] = value
        return bd[0:count * rows, 0:count * cols]

    bp_all = bp16.astype(F32)
    for q in range(A):
        bpq[q] = bp_all[q * CQ:(q + 1) * CQ]
    bq_bd = diagonal(bpq[a], G1).astype(BF16)
    bp_bd = diagonal(bp_all, GROUP).astype(BF16)
    pl_bd = diagonal(pl16.astype(F32), GROUP).astype(BF16)
    wo_bd = wide(split(diagonal(wo_ref[...], GROUP)))
    pr_bd = wide(split(diagonal(pr_ref[...], GROUP)))
    for step in range(1, N):
        peer = lax.rem(me + step, N)
        arrive(r1.at[peer], peer)

    def mix(st, w, width_out):
        mx[...] = jnp.zeros_like(mx)
        for j in range(J):
            for k in range(KZ):
                q = j * KZ + k
                p = J * KZ + q
                re = st[:, q:q + 1]
                im = st[:, p:p + 1]
                wr = w[j, 0, k]
                wi = w[j, 1, k]
                mx[q:q + 1, :width_out] = jnp.sum(re * wr - im * wi, axis=0, keepdims=True)
                mx[p:p + 1, :width_out] = jnp.sum(re * wi + im * wr, axis=0, keepdims=True)
        return mx[...].T[:width_out]

    s4 = jnp.sum(r1[...], axis=0) * scale1
    st = columns[:, 0:1] * s4[0:1]
    for c in range(1, CIN):
        st = st + columns[:, c:c + 1] * s4[c:c + 1]
    first = jnp.where((lane == 0) & (me == 0), gain, 0.0).astype(F32)
    st = st + columns[:, CIN:CIN + 1] * first
    mixed = mix(st, w1, C2)
    for q in range(A):
        mt1[q] = mixed[q * CQ:(q + 1) * CQ]
    g1[me] = mt1[a]

    def group_member(step):
        return own_g * H + lax.rem(own_h + step, H)

    def column(ia, ig):
        return lax.rem(a + ia, A), lax.rem(own_g + ig, IL) * H + own_h

    order = [(ia, ig) for ig in range(IL) for ia in range(A) if ia or ig]
    for ia, ig in reversed(order):
        pa, pb = column(ia, ig)
        remote(mt1.at[pa], g1.at[me], S_EXP1 + me, (pa, pb))
    for t in range(1, H):
        remote(mt1.at[a], g1.at[me], S_EXP1 + me, (a, group_member(t)))

    def fill(value):
        n = value.shape[1]
        high, low = split(value)
        t16[0:CIN, :n] = high.astype(F32)
        t16[CIN:2 * CIN, :n] = low.astype(F32)
        t16[2 * CIN:3 * CIN, :n] = high.astype(F32)
        return t16[:, :n].astype(BF16)

    near_forward(pg, S_POOL)
    for x in range(cells_x):
        fk_ref[x] = fill(f_ref[x * CIN:(x + 1) * CIN])
    near_finish(pg, S_POOL)
    for q in range(A):
        for x in range(hx):
            pk_ref[q * hx + x] = fill(pg[q, x * CIN:(x + 1) * CIN])

    for ia, ig in order:
        pa, pb = column(ia, ig)
        source = pa * B + pb
        arrive(g1.at[source], S_EXP1 + source)
        for t in range(1, H):
            remote(g1.at[source], g1.at[source], S_EXP1 + source, (a, group_member(t)))
    for t in range(1, H):
        for ia, ig in [(0, 0)] + order:
            source = lax.rem(a + ia, A) * B + lax.rem(own_g + ig, IL) * H + lax.rem(own_h + t, H)
            arrive(g1.at[source], S_EXP1 + source)

    l_yic.wait()
    rows = jnp.concatenate(
        [jnp.concatenate([g1[i * H + h] for h in range(H)], axis=1) for i in range(KX)], axis=0
    )
    y = mul3(split(rows), (yic[0], yic[1]))
    for i in range(KX):
        yall[a, i] = y[i * CQ:(i + 1) * CQ]
    near_send(yall, S_Y)

    def modes(value, rows_each):
        groups = rows_each // 8
        turned = rot_i(value)
        parts = []
        for g in range(groups):
            parts.append(jnp.concatenate([
                v[i * rows_each + g * 8:i * rows_each + g * 8 + 8] for v in (value, turned) for i in range(KX)
            ], axis=0))
        return parts

    l_xi.wait()
    table = wide((
        jnp.concatenate([xi[q, 0] for q in range(A)], axis=0),
        jnp.concatenate([xi[q, 1] for q in range(A)], axis=0),
    ))
    v = mul(table, deep(split(jnp.concatenate(modes(y, CQ), axis=1))))
    for s in range(HX // G1):
        vx[s] = jnp.concatenate([
            v[(s * G1 + xx) * 8:(s * G1 + xx) * 8 + 8, g * LB:(g + 1) * LB]
            for xx in range(G1) for g in range(CG)
        ], axis=0)

    def coarse_step(s, carry):
        v = mul(tall(split(vx[s])), tzi_ref[...])
        near = jnp.concatenate([pk_ref[s * G1 + xx] for xx in range(G1)], axis=0)
        g = split(gelu(v + mul(bq_bd, near)))
        zc[s] = mul(tall(g), tzf_ref[...])
        return carry

    l_tzi.wait()
    lax.fori_loop(0, HX // G1, coarse_step, 0)
    near_forward(yall, S_Y)

    l_xf.wait()
    l_yfc.wait()
    z = jnp.concatenate([
        jnp.concatenate([
            zc[s, xx * CQ + g * 8:xx * CQ + g * 8 + 8] for s in range(HX // G1) for xx in range(G1)
        ], axis=0) for g in range(CG)
    ], axis=1)
    z = mul(wide((xf[0], xf[1])), deep(split(z)))
    value = jnp.concatenate([
        z[i * 8:(i + 1) * 8, g * LB:(g + 1) * LB] for i in range(KX) for g in range(CG)
    ], axis=0) + rot_f(jnp.concatenate([
        z[(KX + i) * 8:(KX + i + 1) * 8, g * LB:(g + 1) * LB] for i in range(KX) for g in range(CG)
    ], axis=0))
    out = mul3(split(value), (yfc[0], yfc[1]))
    for i in range(KX):
        for h in range(H):
            buf2[i * H + h] = out[i * CQ:(i + 1) * CQ, h * LB:(h + 1) * LB]
    for step in range(1, N):
        peer = lax.rem(me + step, N)
        remote(buf2.at[peer], r3.at[me], S_RED + me, at(peer))
    r3[me] = buf2[me]

    near_finish(yall, S_Y)
    parts = []
    for q in range(A):
        parts += modes(jnp.concatenate([yall[q, i] for i in range(KX)], axis=0), CQ)
    v = mul(wide((xi[a, 0], xi[a, 1])), deep(split(jnp.concatenate(parts, axis=1))))
    for s in range(hx // GROUP):
        vn[s] = jnp.concatenate([
            v[(s * GROUP + xx) * 8:(s * GROUP + xx) * 8 + 8, g * LB:(g + 1) * LB]
            for xx in range(GROUP) for g in range(C2 // 8)
        ], axis=0)

    def narrow_step(s, carry):
        v = mul(tall(split(vn[s])), tzi_ref[...])
        near = jnp.concatenate([pk_ref[a * hx + s * GROUP + xx] for xx in range(GROUP)], axis=0)
        g = split(gelu(v + mul(bp_bd, near)))
        narrow = mul(wo_bd, deep(g))
        for xx in range(GROUP):
            nar[s * GROUP + xx] = narrow[xx * C1:(xx + 1) * C1]
        return carry

    lax.fori_loop(0, hx // GROUP, narrow_step, 0)

    l_w2.wait()
    for step in range(1, N):
        peer = lax.rem(me + step, N)
        arrive(r3.at[peer], S_RED + peer)
    sums = []
    for q in range(A):
        total = r3[q * B]
        for t in range(1, B):
            total = total + r3[q * B + t]
        sums.append(total)
    st = (jnp.concatenate(sums, axis=0) * scale2).T
    mixed = jnp.zeros((C1, LB), F32)
    for j in range(J):
        for k in range(KZ):
            q = j * KZ + k
            p = J * KZ + q
            re = st[q:q + 1]
            im = st[p:p + 1]
            wr = w2[j, 0, k]
            wi = w2[j, 1, k]
            real = jnp.sum(re * wr - im * wi, axis=1, keepdims=True)
            imag = jnp.sum(re * wi + im * wr, axis=1, keepdims=True)
            mixed = jnp.where(lane == q, real, jnp.where(lane == p, imag, mixed))
    ag2[me] = mixed

    def flip(t):
        value = b
        bit = 1
        while bit < B:
            if t & bit:
                value = value + bit - 2 * bit * lax.rem(b // bit, 2)
            bit *= 2
        return value

    def spread(source):
        for peer in mates + [sib]:
            remote(ag2.at[source], ag2.at[source], S_EXP2 + source, (peer, b))

    for t in range(B - 1, 0, -1):
        remote(ag2.at[me], ag2.at[me], S_EXP2 + me, (a, flip(t)))
    spread(me)
    for t in range(1, B):
        source = a * B + flip(t)
        arrive(ag2.at[source], S_EXP2 + source)
        spread(source)
    for t in range(B):
        for peer in mates:
            source = peer * B + flip(t)
            arrive(ag2.at[source], S_EXP2 + source)
            remote(ag2.at[source], ag2.at[source], S_EXP2 + source, (sib, b))
    for t in range(B):
        for peer in [a] + mates:
            source = (peer + 1 - 2 * core) * B + flip(t)
            arrive(ag2.at[source], S_EXP2 + source)

    l_yi2.wait()
    l_xo.wait()
    rows = jnp.concatenate(
        [jnp.concatenate([ag2[i * H + h] for h in range(H)], axis=1) for i in range(KX)], axis=0
    )
    y = mul3(split(rows), (yi2[0], yi2[1]))
    halves_y = [modes(y[:, ch * LB:(ch + 1) * LB], C1) for ch in range(2)]
    v = mul(wide((xo[0], xo[1])), deep(split(jnp.concatenate(halves_y[0] + halves_y[1], axis=1))))
    CF = C1 // 8
    for s in range(cells_x // GROUP):
        for ch in range(2):
            vf[s, ch] = jnp.concatenate([
                v[(s * GROUP + xx) * 8:(s * GROUP + xx) * 8 + 8, (ch * CF + g) * LB:(ch * CF + g + 1) * LB]
                for xx in range(GROUP) for g in range(CF)
            ], axis=0)

    def fine_step(group, carry):
        near = jnp.concatenate([fk_ref[group * GROUP + xx] for xx in range(GROUP)], axis=0)
        for ch in range(2):
            v = mul(tall(split(vf[group, ch])), tzi_ref[...])
            rows = []
            for xx in range(0, GROUP, 2):
                half = nar.at[group * (GROUP // 2) + xx // 2]
                pieces = []
                for yy in range(YB):
                    at_y = (ch * YB + yy) // 2 * zn
                    pieces.append(half[:, at_y:at_y + zn])
                rows += [jnp.concatenate(pieces, axis=1) + bo_col] * 2
            g = split(gelu(v + jnp.concatenate(rows, axis=0)))
            cols = slice(ch * width, (ch + 1) * width)
            res = mul(pr_bd, deep(g)) + mul(pl_bd, near[:, cols])
            for xx in range(GROUP):
                o_ref[group * GROUP + xx, :, cols] = res[xx * CIN:(xx + 1) * CIN]
        return carry

    lax.fori_loop(0, cells_x // GROUP, fine_step, 0)
    for copy in sends:
        copy.wait_send()


def on_device(
    A, B, fields, lift, lift_bias, spectral_in, bypass_in, bias_in, spectral_out, bypass_out,
    bias_out, proj, proj_bias,
):
    cin, xc, yc, zc = fields.shape
    C1 = lift.shape[0]
    C2 = bypass_in.shape[0]
    NX = xc * A
    NY = yc * B
    IL = KX // A
    H = B // IL
    J = KY // H
    N = A * B
    width = YB * zc
    CQ = C2 // A
    hx = xc // 2
    HX = hx * A
    G1 = GROUP * C2 // CQ
    cells = float(NX * NY * zc)
    back = math.sqrt(2.0 / (KX * KY * KZ))

    tz = z_table(zc)
    tzf = stacked(tz)
    tzi = stacked(np.ascontiguousarray(tz.T) * back)
    fine_x = x_angles(A, xc, NX)
    half_x = x_angles(A, xc // 2, NX // 2)
    eye = np.eye(cin)
    tx = np.stack([
        np.concatenate([np.kron(np.cos(fine_x[i].T), eye), np.kron(np.sin(fine_x[i].T), eye)], axis=1)
        for i in range(A)
    ])
    eye8 = np.eye(8)

    def lines(ang):
        return np.concatenate([np.kron(np.cos(ang), eye8), np.kron(np.sin(ang), eye8)], axis=1)

    xi = np.stack([lines(half_x[i]) for i in range(A)])
    xf = np.ascontiguousarray(xi.reshape(-1, xi.shape[2]).T)
    xo = np.stack([lines(fine_x[i]) for i in range(A)])
    yf1 = y_table(B, yc, NY, H)
    yfc = y_table(B, yc // 2, NY // 2, H)

    def per_device(table):
        return jnp.asarray(np.ascontiguousarray(np.swapaxes(halves(table), 0, 1)))

    tx_t = per_device(tx)
    yf1_t = per_device(yf1)
    yfc_t = per_device(yfc)
    yic_t = per_device(np.swapaxes(yfc, 1, 2))
    yi2_t = per_device(np.swapaxes(yf1, 1, 2))
    xi_t = per_device(xi)
    xo_t = per_device(xo)
    xf_t = jnp.asarray(halves(xf))

    rows = jnp.transpose(fields, (1, 0, 2, 3)).reshape(xc * cin, yc * zc)
    weights2 = jnp.swapaxes(spectral_out, 3, 4)

    vmem = pl.BlockSpec(memory_space=pltpu.VMEM)
    anywhere = pl.BlockSpec(memory_space=pl.ANY)
    V = pltpu.VMEM
    out = pl.pallas_call(
        functools.partial(
            kernel, A, B, xc, 1.0 / math.sqrt(cells), 1.0 / math.sqrt(cells / 4.0), math.sqrt(cells)
        ),
        out_shape=jax.ShapeDtypeStruct((xc, cin, yc * zc), F32),
        in_specs=[vmem] * 10 + [anywhere] * 11,
        out_specs=vmem,
        scratch_shapes=[
            V(tzi.shape, BF16), V(spectral_in.shape, F32), V(weights2.shape, F32),
            V(tx_t.shape[1:], BF16), V(yf1_t.shape[1:], BF16), V(yfc_t.shape[1:], BF16),
            V(yic_t.shape[1:], BF16), V(yi2_t.shape[1:], BF16), V(xf_t.shape, BF16), V(xi_t.shape, BF16),
            V(xo_t.shape[1:], BF16),
            V((N, cin, LB), F32), V((N, cin, LB), F32), V((LB, LB), F32),
            V((A, CQ, LB), F32), V((N, CQ, LB), F32), V((A, KX, CQ, LB), F32),
            V((A, hx * cin, width), F32), V((hx * A, 16, width), BF16),
            V((HX // G1, G1 * CQ, LB), F32), V((HX // G1, G1 * CQ, LB), F32), V((hx // GROUP, GROUP * C2, LB), F32),
            V((N, CQ, LB), F32), V((N, CQ, LB), F32), V((N, C1, LB), F32),
            V((xc // GROUP, 2, GROUP * C1, LB), F32),
            V((hx, C1, width), F32), V((xc, 16, yc * zc), BF16), V((16, yc * zc), F32),
            V((GROUP * C2, max(GROUP * C2, G1 * 16)), F32), V((A, CQ, 16), F32),
            pltpu.SemaphoreType.DMA((11,)),
            pltpu.SemaphoreType.DMA((4 * N + 2 * A,)), pltpu.SemaphoreType.DMA((4 * N + 2 * A,)),
        ],
        compiler_params=pltpu.CompilerParams(
            collective_id=0, has_side_effects=True, vmem_limit_bytes=60 * 1024 * 1024
        ),
    )(
        rows, lift.T, lift_bias[None], bypass_in.T, bias_in[None], bypass_out, bias_out[None], proj,
        proj_bias[None], jnp.asarray(tzf),
        jnp.asarray(tzi), spectral_in, weights2, tx_t, yf1_t, yfc_t, yic_t, yi2_t, xf_t, xi_t, xo_t,
    )
    return jnp.transpose(out.reshape(xc, cin, yc, zc), (1, 0, 2, 3))


def solution(mesh):
    A = mesh.shape["gx"]
    B = mesh.shape["gy"]
    in_specs = (
        P(None, "gx", "gy", None), P(), P(), P(("gx", "gy"), None, None, None, None), P(), P(),
        P(("gx", "gy"), None, None, None, None), P(), P(), P(), P(),
    )
    return jax.shard_map(
        functools.partial(on_device, A, B), mesh=mesh, in_specs=in_specs,
        out_specs=P(None, "gx", "gy", None), check_vma=False,
    )
```

time: 64.7 us -> 55.4 us (0.86)
  Pallas kernels: 60.3 us -> 50.3 us
    pallas_call x1, Pallas kernels: 60.3 us -> 50.3 us  [on_device(): pl.pallas_call(functools.partial(kernel, A, B, xc, 1.0 / math.sqrt(cells)...]
where the time goes in v1:
time: 55.4 us; the launch traced here: 54.5 us
  Pallas kernels  50.3 us (91%)
  local copies, waits for them, and re-layouts  4.19 us (8%)
    pallas_call x1, Pallas kernels, on_device(): pl.pallas_call(functools.partial(kernel, A, B, xc, 1.0 / math.sqrt(cells)...  50.3 us
    reshape x2, local copies, waits for them, and re-layouts, on_device(): return jnp.transpose(out.reshape(xc, cin, yc, zc), (1, 0, 2, 3))  2.15 us

profile of v1, /device:TPU:0, one launch (start us, length us, event | category | flops | bytes accessed | tf_op | source)
XLA Modules:
  0.0 54.5 jit_solution(7472799758198551291)
XLA Ops:
  0.0 1.1 %copy.22 = f32[16,4,16,128]{3,2,1,0:T(8,128)S(1)} copy(f32[16,4,16,128]{3,2,0,1:T(8,128)} %bitcast.19) | data formatting | bytes 1048576 | tf_op jit(solution)/shard_map/transpose | solution.py:582
  1.1 1.0 %copy.27 = f32[8,8,16,128]{3,1,2,0:T(8,128)} copy(f32[8,8,16,128]{3,2,1,0:T(8,128)S(1)} %bitcast.17) | data formatting | bytes 1048576
  2.0 50.3 %shard_map.199 = f32[16,4,2048]{2,1,0:T(4,128)} custom-call(f32[64,2048]{1,0:T(8,128)} %bitcast.16, f32[4,32]{1,0:T(4,128)} %bitcast.21, f32[1,32]{1,0:T(1,128)} %bitcast.22, f32[32,64]{1,0:T(8,128)} %bitcast.20, f32[1,64]{1,0:T(1,128)} %bitcast.23, f32[32,64]{1,0:T(8,128)} %wo_ref.1, f32[1,32]{1,0:T(1,128)} %bitcast.24, f32[4,32]{1,0:T(4,128)} %pr_ref.1, ...), custom_call_target="tpu_custom_call" | custom-call | tf_op jit(solution)/shard_map/pallas_call | solution.py:588
  52.4 1.3 %reshape.7 = f32[16,4,16,128]{3,2,1,0:T(8,128)S(1)} reshape(f32[16,4,2048]{2,1,0:T(4,128)} %shard_map.199) | data formatting | bytes 1048576 | tf_op jit(solution)/shard_map/reshape | solution.py:619
  53.7 0.8 %copy.28 = f32[16,4,16,128]{3,2,0,1:T(8,128)} copy(f32[16,4,16,128]{3,2,1,0:T(8,128)S(1)} %reshape.7) | data formatting | bytes 1048576 | tf_op jit(solution)/shard_map/reshape | solution.py:619

commit v2 on v1

--- a/solution.py
+++ b/solution.py
@@ -104,13 +104,13 @@
 
 
 def kernel(
-    A, B, cells_x, scale1, scale2, gain,
-    f_ref, lift_ref, lbias_ref, byp_ref, bi_ref, wo_ref, bo_ref, pr_ref, pb_ref,
-    tzf_ref, tzi_hbm, w1_hbm, w2_hbm, tx_hbm, yf1_hbm, yfc_hbm, yic_hbm, yi2_hbm, xf_hbm, xi_hbm, xo_hbm,
+    A, B, cells_x, cells_y, scale1, scale2, gain,
+    f_hbm, lift_hbm, lbias_hbm, byp_hbm, bi_hbm, wo_hbm, bo_hbm, pr_hbm, pb_hbm, tzf_hbm, tzi_hbm, w1_hbm, w2_hbm, tx_hbm, yf1_hbm, yfc_hbm, yic_hbm, yi2_hbm, xf_hbm, xi_hbm, xo_hbm,
     o_ref,
+    fx, f_ref, lift_ref, lbias_ref, byp_ref, bi_ref, wo_ref, bo_ref, pr_ref, pb_ref, tzf_ref, os_ref,
     tzi_ref, w1, w2, tx, yf1, yfc, yic, yi2, xf, xi, xo,
-    buf1, r1, mx, mt1, g1, yall, pg, pk_ref, vx, zc, vn, buf2, r3, ag2, vf, nar, fk_ref, t16, bd, bpq,
-    csem, ssem, rsem,
+    buf1, r1, mx, mt1, r5, buf5, yall, pg, pk_ref, vx, zc, vn, buf2, r3, buf4, r4, ag2, vf, nar, fk_ref, t16, bd, bpq,
+    fsem, csem, ssem, rsem,
 ):
     a = lax.axis_index("gx")
     b = lax.axis_index("gy")
@@ -131,15 +131,17 @@
     own_h = lax.rem(b, H)
     core = lax.rem(a, 2)
     sib = a + 1 - 2 * core
-    mates = [lax.rem(a + 2 * s, A) for s in range(1, X)]
-
+
+    fields = [pltpu.make_async_copy(f_hbm.at[c], fx.at[:, c], fsem.at[c]) for c in range(CIN)]
     pairs = [
-        (tx_hbm.at[a], tx), (yf1_hbm.at[b], yf1), (w1_hbm, w1), (yic_hbm.at[b], yic), (xi_hbm, xi), (tzi_hbm, tzi_ref),
-        (xf_hbm, xf), (yfc_hbm.at[b], yfc), (w2_hbm, w2), (yi2_hbm.at[b], yi2), (xo_hbm.at[a], xo),
-    ]
+        (tzf_hbm, tzf_ref), (tx_hbm.at[a], tx), (yf1_hbm.at[b], yf1), (lift_hbm, lift_ref), (lbias_hbm, lbias_ref),
+        (byp_hbm, byp_ref), (bi_hbm, bi_ref), (wo_hbm, wo_ref), (bo_hbm, bo_ref), (pr_hbm, pr_ref), (pb_hbm, pb_ref),
+        (w1_hbm, w1), (xi_hbm, xi), (tzi_hbm, tzi_ref), (xf_hbm, xf), (w2_hbm, w2), (yi2_hbm.at[b], yi2), (xo_hbm.at[a], xo),
+    ] + [(yic_hbm.at[g * H + own_h], yic.at[g]) for g in range(IL)] + [(yfc_hbm.at[g * H + own_h], yfc.at[g]) for g in range(IL)]
     loads = [pltpu.make_async_copy(src, dst, csem.at[k]) for k, (src, dst) in enumerate(pairs)]
-    l_tx, l_yf1, l_w1, l_yic, l_xi, l_tzi, l_xf, l_yfc, l_w2, l_yi2, l_xo = loads
-    for load in loads:
+    l_tzf, l_tx, l_yf1 = loads[:3]
+    l_w1, l_xi, l_tzi, l_xf, l_w2, l_yi2, l_xo = loads[11:18]
+    for load in fields + loads[:3]:
         load.start()
 
     barrier = pltpu.get_barrier_semaphore()
@@ -148,6 +150,8 @@
         pl.semaphore_signal(
             barrier, inc=1, device_id=(peer // B, lax.rem(peer, B)), device_id_type=MESH
         )
+    for load in loads[3:]:
+        load.start()
 
     lane = lax.broadcasted_iota(jnp.int32, (1, LB), 1)
     sign_f = jnp.where(lane < LB // 2, 1.0, -1.0).astype(F32)
@@ -158,30 +162,36 @@
     def rot_i(v):
         return pltpu.roll(v, LB // 2, 1) * -sign_f
 
-    sends = []
-    used = [0]
-
-    def remote(source, target, slot, device):
-        copy = pltpu.make_async_remote_copy(
-            src_ref=source, dst_ref=target, send_sem=ssem.at[used[0]], recv_sem=rsem.at[slot],
+    def remote(source, target, phase, slot, device):
+        pltpu.make_async_remote_copy(
+            src_ref=source, dst_ref=target, send_sem=ssem.at[phase], recv_sem=rsem.at[slot],
             device_id=device, device_id_type=MESH,
+        ).start()
+
+    def whole(target, phase, slot):
+        return pltpu.make_async_remote_copy(
+            src_ref=target, dst_ref=target, send_sem=ssem.at[phase], recv_sem=rsem.at[slot],
+            device_id=(sib, b), device_id_type=MESH,
         )
-        used[0] += 1
-        copy.start()
-        sends.append(copy)
 
     def arrive(target, slot):
-        pltpu.make_async_remote_copy(
-            src_ref=target, dst_ref=target, send_sem=ssem.at[0], recv_sem=rsem.at[slot],
-            device_id=(sib, b), device_id_type=MESH,
-        ).wait_recv()
+        whole(target, 0, slot).wait_recv()
 
     def at(index):
         return (index // B, lax.rem(index, B))
 
-    S_EXP1, S_RED, S_EXP2, S_POOL, S_Y = N, 2 * N, 3 * N, 4 * N, 4 * N + A
+    A2A, PAIR1, EXP1, RED, PAIR2, EXP2, POOL, YALL = range(8)
+    SPREAD = 8
+    NEAR = SPREAD + X * B
 
     width = tzi_ref.shape[1]
+    for load in fields:
+        load.wait()
+    flat = fx.reshape(f_ref.shape[0] * cells_y, f_ref.shape[1] // cells_y)
+    zn = flat.shape[1]
+    for y in range(cells_y):
+        f_ref[:, y * zn:(y + 1) * zn] = flat[pl.ds(y, f_ref.shape[0], stride=cells_y), :]
+    l_tzf.wait()
     zs = []
     for ch in range(2):
         zs.append(mul(tall(split(f_ref[:, ch * width:(ch + 1) * width])), tzf_ref[...]))
@@ -199,9 +209,8 @@
 
     for step in range(1, N):
         peer = lax.rem(me + step, N)
-        remote(buf1.at[peer], r1.at[me], me, at(peer))
-
-    zn = width // YB
+        remote(buf1.at[peer], r1.at[me], A2A, A2A, at(peer))
+
     for x in range(hx):
         both = f_ref[2 * x * CIN:(2 * x + 1) * CIN] + f_ref[(2 * x + 1) * CIN:(2 * x + 2) * CIN]
         pieces = [
@@ -210,24 +219,27 @@
         ]
         pg[a, x * CIN:(x + 1) * CIN] = jnp.concatenate(pieces, axis=1) * 0.25
 
-    def near_send(buffer, slot):
-        for peer in mates + [sib]:
-            remote(buffer.at[a], buffer.at[a], slot + a, (peer, b))
-
-    def near_forward(buffer, slot):
-        for peer in mates:
-            arrive(buffer.at[peer], slot + peer)
-            remote(buffer.at[peer], buffer.at[peer], slot + peer, (sib, b))
-
-    def near_finish(buffer, slot):
-        arrive(buffer.at[sib], slot + sib)
-        for peer in mates:
-            other = peer + 1 - 2 * core
-            arrive(buffer.at[other], slot + other)
-
-    near_send(pg, S_POOL)
-
-    l_w1.wait()
+    def near_slot(phase, step):
+        return NEAR + (phase - POOL) * X + step
+
+    def near_send(buffer, phase):
+        for step in range(1, X):
+            remote(buffer.at[a], buffer.at[a], phase, near_slot(phase, step), (lax.rem(a + 2 * step, A), b))
+        remote(buffer.at[a], buffer.at[a], phase, phase, (sib, b))
+
+    def near_forward(buffer, phase):
+        for step in range(1, X):
+            peer = lax.rem(a + A - 2 * step, A)
+            arrive(buffer.at[peer], near_slot(phase, step))
+            remote(buffer.at[peer], buffer.at[peer], phase, phase, (sib, b))
+
+    def near_finish(buffer, phase):
+        arrive(buffer.at[pl.ds(0, X)], phase)
+
+    near_send(pg, POOL)
+
+    for load in loads[3:12]:
+        load.wait()
     mx[...] = jnp.zeros_like(mx)
     mx[0:CIN, :C1] = lift_ref[...]
     mx[CIN:CIN + 1, :C1] = lbias_ref[...]
@@ -275,9 +287,7 @@
     pl_bd = diagonal(pl16.astype(F32), GROUP).astype(BF16)
     wo_bd = wide(split(diagonal(wo_ref[...], GROUP)))
     pr_bd = wide(split(diagonal(pr_ref[...], GROUP)))
-    for step in range(1, N):
-        peer = lax.rem(me + step, N)
-        arrive(r1.at[peer], peer)
+    arrive(r1.at[pl.ds(0, N - 1)], A2A)
 
     def mix(st, w, width_out):
         mx[...] = jnp.zeros_like(mx)
@@ -300,9 +310,8 @@
     first = jnp.where((lane == 0) & (me == 0), gain, 0.0).astype(F32)
     st = st + columns[:, CIN:CIN + 1] * first
     mixed = mix(st, w1, C2)
-    for q in range(A):
-        mt1[q] = mixed[q * CQ:(q + 1) * CQ]
-    g1[me] = mt1[a]
+    mt1[...] = mixed
+    r5[own_h] = mixed
 
     def group_member(step):
         return own_g * H + lax.rem(own_h + step, H)
@@ -311,11 +320,8 @@
         return lax.rem(a + ia, A), lax.rem(own_g + ig, IL) * H + own_h
 
     order = [(ia, ig) for ig in range(IL) for ia in range(A) if ia or ig]
-    for ia, ig in reversed(order):
-        pa, pb = column(ia, ig)
-        remote(mt1.at[pa], g1.at[me], S_EXP1 + me, (pa, pb))
     for t in range(1, H):
-        remote(mt1.at[a], g1.at[me], S_EXP1 + me, (a, group_member(t)))
+        remote(mt1, r5.at[own_h], PAIR1, PAIR1, (a, group_member(t)))
 
     def fill(value):
         n = value.shape[1]
@@ -325,33 +331,30 @@
         t16[2 * CIN:3 * CIN, :n] = high.astype(F32)
         return t16[:, :n].astype(BF16)
 
-    near_forward(pg, S_POOL)
     for x in range(cells_x):
         fk_ref[x] = fill(f_ref[x * CIN:(x + 1) * CIN])
-    near_finish(pg, S_POOL)
+    near_forward(pg, POOL)
+    for load in loads[18:18 + IL]:
+        load.wait()
+    arrive(r5.at[pl.ds(0, H - 1)], PAIR1)
+    rows = jnp.concatenate([r5[h] for h in range(H)], axis=1)
+    tables = tuple(jnp.concatenate([yic[g, n] for g in range(IL)], axis=1) for n in range(2))
+    y = mul3(split(rows), tables)
+    for q in range(A):
+        for g in range(IL):
+            buf5[q * IL + g] = y[q * CQ:(q + 1) * CQ, g * LB:(g + 1) * LB]
+    mine = a * IL + own_g
+    for ia, ig in reversed(order):
+        pa, pb = column(ia, ig)
+        remote(buf5.at[pa * IL + pb // H], yall.at[pa, mine], EXP1, EXP1, (pa, pb))
+    yall[a, mine] = buf5[mine]
+    near_finish(pg, POOL)
     for q in range(A):
         for x in range(hx):
             pk_ref[q * hx + x] = fill(pg[q, x * CIN:(x + 1) * CIN])
-
-    for ia, ig in order:
-        pa, pb = column(ia, ig)
-        source = pa * B + pb
-        arrive(g1.at[source], S_EXP1 + source)
-        for t in range(1, H):
-            remote(g1.at[source], g1.at[source], S_EXP1 + source, (a, group_member(t)))
-    for t in range(1, H):
-        for ia, ig in [(0, 0)] + order:
-            source = lax.rem(a + ia, A) * B + lax.rem(own_g + ig, IL) * H + lax.rem(own_h + t, H)
-            arrive(g1.at[source], S_EXP1 + source)
-
-    l_yic.wait()
-    rows = jnp.concatenate(
-        [jnp.concatenate([g1[i * H + h] for h in range(H)], axis=1) for i in range(KX)], axis=0
-    )
-    y = mul3(split(rows), (yic[0], yic[1]))
-    for i in range(KX):
-        yall[a, i] = y[i * CQ:(i + 1) * CQ]
-    near_send(yall, S_Y)
+    arrive(yall.at[a, pl.ds(0, KX - 1)], EXP1)
+    near_send(yall, YALL)
+    y = jnp.concatenate([yall[a, i] for i in range(KX)], axis=0)
 
     def modes(value, rows_each):
         groups = rows_each // 8
@@ -384,10 +387,8 @@
 
     l_tzi.wait()
     lax.fori_loop(0, HX // G1, coarse_step, 0)
-    near_forward(yall, S_Y)
 
     l_xf.wait()
-    l_yfc.wait()
     z = jnp.concatenate([
         jnp.concatenate([
             zc[s, xx * CQ + g * 8:xx * CQ + g * 8 + 8] for s in range(HX // G1) for xx in range(G1)
@@ -399,16 +400,15 @@
     ], axis=0) + rot_f(jnp.concatenate([
         z[(KX + i) * 8:(KX + i + 1) * 8, g * LB:(g + 1) * LB] for i in range(KX) for g in range(CG)
     ], axis=0))
-    out = mul3(split(value), (yfc[0], yfc[1]))
     for i in range(KX):
-        for h in range(H):
-            buf2[i * H + h] = out[i * CQ:(i + 1) * CQ, h * LB:(h + 1) * LB]
-    for step in range(1, N):
-        peer = lax.rem(me + step, N)
-        remote(buf2.at[peer], r3.at[me], S_RED + me, at(peer))
-    r3[me] = buf2[me]
-
-    near_finish(yall, S_Y)
+        buf2[i] = value[i * CQ:(i + 1) * CQ]
+    for ia, ig in reversed(order):
+        pa, pb = column(ia, ig)
+        remote(buf2.at[pa * IL + pb // H], r3.at[a * IL + own_g], RED, RED, (pa, pb))
+    r3[a * IL + own_g] = buf2[a * IL + own_g]
+
+    near_forward(yall, YALL)
+    near_finish(yall, YALL)
     parts = []
     for q in range(A):
         parts += modes(jnp.concatenate([yall[q, i] for i in range(KX)], axis=0), CQ)
@@ -431,16 +431,22 @@
     lax.fori_loop(0, hx // GROUP, narrow_step, 0)
 
     l_w2.wait()
-    for step in range(1, N):
-        peer = lax.rem(me + step, N)
-        arrive(r3.at[peer], S_RED + peer)
-    sums = []
-    for q in range(A):
-        total = r3[q * B]
-        for t in range(1, B):
-            total = total + r3[q * B + t]
-        sums.append(total)
-    st = (jnp.concatenate(sums, axis=0) * scale2).T
+    for load in loads[18 + IL:]:
+        load.wait()
+    arrive(r3.at[pl.ds(0, KX - 1)], RED)
+    value = jnp.concatenate(
+        [jnp.concatenate([r3[q * IL + g] for g in range(IL)], axis=1) for q in range(A)], axis=0
+    )
+    tables = tuple(jnp.concatenate([yfc[g, n] for g in range(IL)], axis=0) for n in range(2))
+    out = mul3(split(value), tables)
+    for h in range(H):
+        buf4[h] = out[:, h * LB:(h + 1) * LB]
+    for t in range(1, H):
+        peer = lax.rem(own_h + t, H)
+        remote(buf4.at[peer], r4.at[own_h], PAIR2, PAIR2, (a, group_member(t)))
+    r4[own_h] = buf4[own_h]
+    arrive(r4.at[pl.ds(0, H - 1)], PAIR2)
+    st = (jnp.sum(r4[...], axis=0) * scale2).T
     mixed = jnp.zeros((C1, LB), F32)
     for j in range(J):
         for k in range(KZ):
@@ -464,26 +470,27 @@
             bit *= 2
         return value
 
-    def spread(source):
-        for peer in mates + [sib]:
-            remote(ag2.at[source], ag2.at[source], S_EXP2 + source, (peer, b))
+    def spread(t):
+        source = a * B + flip(t)
+        for step in range(1, X):
+            remote(
+                ag2.at[source], ag2.at[source], EXP2, SPREAD + step * B + t, (lax.rem(a + 2 * step, A), b)
+            )
+        remote(ag2.at[source], ag2.at[source], EXP2, EXP2, (sib, b))
 
     for t in range(B - 1, 0, -1):
-        remote(ag2.at[me], ag2.at[me], S_EXP2 + me, (a, flip(t)))
-    spread(me)
+        remote(ag2.at[me], ag2.at[me], EXP2, SPREAD + t, (a, flip(t)))
+    spread(0)
     for t in range(1, B):
         source = a * B + flip(t)
-        arrive(ag2.at[source], S_EXP2 + source)
-        spread(source)
+        arrive(ag2.at[source], SPREAD + t)
+        spread(t)
     for t in range(B):
-        for peer in mates:
-            source = peer * B + flip(t)
-            arrive(ag2.at[source], S_EXP2 + source)
-            remote(ag2.at[source], ag2.at[source], S_EXP2 + source, (sib, b))
-    for t in range(B):
-        for peer in [a] + mates:
-            source = (peer + 1 - 2 * core) * B + flip(t)
-            arrive(ag2.at[source], S_EXP2 + source)
+        for step in range(1, X):
+            source = lax.rem(a + A - 2 * step, A) * B + flip(t)
+            arrive(ag2.at[source], SPREAD + step * B + t)
+            remote(ag2.at[source], ag2.at[source], EXP2, EXP2, (sib, b))
+    arrive(ag2.at[pl.ds(0, X * B)], EXP2)
 
     l_yi2.wait()
     l_xo.wait()
@@ -516,13 +523,22 @@
             g = split(gelu(v + jnp.concatenate(rows, axis=0)))
             cols = slice(ch * width, (ch + 1) * width)
             res = mul(pr_bd, deep(g)) + mul(pl_bd, near[:, cols])
+            for yy in range(YB):
+                os_ref[ch, yy * GROUP * CIN:(yy + 1) * GROUP * CIN] = res[:, yy * zn:(yy + 1) * zn]
             for xx in range(GROUP):
-                o_ref[group * GROUP + xx, :, cols] = res[xx * CIN:(xx + 1) * CIN]
+                for c in range(CIN):
+                    o_ref[c, group * GROUP + xx, ch * YB:(ch + 1) * YB] = os_ref[
+                        ch, pl.ds(xx * CIN + c, YB, stride=GROUP * CIN), :
+                    ]
         return carry
 
     lax.fori_loop(0, cells_x // GROUP, fine_step, 0)
-    for copy in sends:
-        copy.wait_send()
+    for phase, target in (
+        (A2A, buf1.at[pl.ds(0, N - 1)]), (PAIR1, r5.at[pl.ds(0, H - 1)]), (EXP1, buf5.at[pl.ds(0, KX - 1)]),
+        (RED, buf2.at[pl.ds(0, KX - 1)]), (PAIR2, buf4.at[pl.ds(0, H - 1)]), (EXP2, ag2.at[pl.ds(0, N - 1)]),
+        (POOL, pg.at[pl.ds(0, A - 1)]), (YALL, yall.at[pl.ds(0, A - 1)]),
+    ):
+        whole(target, phase, phase).wait_send()
 
 
 def on_device(
@@ -579,44 +595,46 @@
     xo_t = per_device(xo)
     xf_t = jnp.asarray(halves(xf))
 
-    rows = jnp.transpose(fields, (1, 0, 2, 3)).reshape(xc * cin, yc * zc)
     weights2 = jnp.swapaxes(spectral_out, 3, 4)
 
-    vmem = pl.BlockSpec(memory_space=pltpu.VMEM)
+    operands = [
+        fields, lift.T, lift_bias[None], bypass_in.T, bias_in[None], bypass_out, bias_out[None], proj,
+        proj_bias[None], jnp.asarray(tzf),
+        jnp.asarray(tzi), spectral_in, weights2, tx_t, yf1_t, yfc_t, yic_t, yi2_t, xf_t, xi_t, xo_t,
+    ]
     anywhere = pl.BlockSpec(memory_space=pl.ANY)
     V = pltpu.VMEM
-    out = pl.pallas_call(
+    return pl.pallas_call(
         functools.partial(
-            kernel, A, B, xc, 1.0 / math.sqrt(cells), 1.0 / math.sqrt(cells / 4.0), math.sqrt(cells)
+            kernel, A, B, xc, yc, 1.0 / math.sqrt(cells), 1.0 / math.sqrt(cells / 4.0), math.sqrt(cells)
         ),
-        out_shape=jax.ShapeDtypeStruct((xc, cin, yc * zc), F32),
-        in_specs=[vmem] * 10 + [anywhere] * 11,
-        out_specs=vmem,
+        out_shape=pltpu.VMEM((cin, xc, yc, zc), F32),
+        in_specs=[anywhere] * len(operands),
+        out_specs=pl.BlockSpec(memory_space=pltpu.VMEM),
         scratch_shapes=[
+            V((xc, cin, yc, zc), F32), V((xc * cin, yc * zc), F32),
+        ] + [V(v.shape, v.dtype) for v in operands[1:10]] + [
+            V((2, YB * GROUP * cin, zc), F32),
             V(tzi.shape, BF16), V(spectral_in.shape, F32), V(weights2.shape, F32),
-            V(tx_t.shape[1:], BF16), V(yf1_t.shape[1:], BF16), V(yfc_t.shape[1:], BF16),
-            V(yic_t.shape[1:], BF16), V(yi2_t.shape[1:], BF16), V(xf_t.shape, BF16), V(xi_t.shape, BF16),
+            V(tx_t.shape[1:], BF16), V(yf1_t.shape[1:], BF16), V((IL,) + yfc_t.shape[1:], BF16),
+            V((IL,) + yic_t.shape[1:], BF16), V(yi2_t.shape[1:], BF16), V(xf_t.shape, BF16), V(xi_t.shape, BF16),
             V(xo_t.shape[1:], BF16),
             V((N, cin, LB), F32), V((N, cin, LB), F32), V((LB, LB), F32),
-            V((A, CQ, LB), F32), V((N, CQ, LB), F32), V((A, KX, CQ, LB), F32),
+            V((C2, LB), F32), V((H, C2, LB), F32), V((KX, CQ, LB), F32), V((A, KX, CQ, LB), F32),
             V((A, hx * cin, width), F32), V((hx * A, 16, width), BF16),
             V((HX // G1, G1 * CQ, LB), F32), V((HX // G1, G1 * CQ, LB), F32), V((hx // GROUP, GROUP * C2, LB), F32),
-            V((N, CQ, LB), F32), V((N, CQ, LB), F32), V((N, C1, LB), F32),
+            V((KX, CQ, LB), F32), V((KX, CQ, LB), F32), V((H, C2, LB), F32), V((H, C2, LB), F32), V((N, C1, LB), F32),
             V((xc // GROUP, 2, GROUP * C1, LB), F32),
             V((hx, C1, width), F32), V((xc, 16, yc * zc), BF16), V((16, yc * zc), F32),
             V((GROUP * C2, max(GROUP * C2, G1 * 16)), F32), V((A, CQ, 16), F32),
-            pltpu.SemaphoreType.DMA((11,)),
-            pltpu.SemaphoreType.DMA((4 * N + 2 * A,)), pltpu.SemaphoreType.DMA((4 * N + 2 * A,)),
+            pltpu.SemaphoreType.DMA((cin,)),
+            pltpu.SemaphoreType.DMA((18 + 2 * IL,)),
+            pltpu.SemaphoreType.DMA((8,)), pltpu.SemaphoreType.DMA((8 + A * B // 2 + A,)),
         ],
         compiler_params=pltpu.CompilerParams(
             collective_id=0, has_side_effects=True, vmem_limit_bytes=60 * 1024 * 1024
         ),
-    )(
-        rows, lift.T, lift_bias[None], bypass_in.T, bias_in[None], bypass_out, bias_out[None], proj,
-        proj_bias[None], jnp.asarray(tzf),
-        jnp.asarray(tzi), spectral_in, weights2, tx_t, yf1_t, yfc_t, yic_t, yi2_t, xf_t, xi_t, xo_t,
-    )
-    return jnp.transpose(out.reshape(xc, cin, yc, zc), (1, 0, 2, 3))
+    )(*operands)
 
 
 def solution(mesh):

time: 55.4 us -> 46.2 us (0.83)
  Pallas kernels: 50.3 us -> 44.6 us
  local copies, waits for them, and re-layouts: 4.19 us -> 0.8 us
    pallas_call x1, Pallas kernels: 50.3 us -> 44.6 us  [on_device(): pl.pallas_call(functools.partial(kernel, A, B, xc, yc, 1.0 / math.sqrt(ce...]
    reshape x2 -> x0, local copies, waits for them, and re-layouts: 2.15 us -> none  [on_device(): return jnp.transpose(out.reshape(xc, cin, yc, zc), (1, 0, 2, 3))]
    transpose x1 -> x0, local copies, waits for them, and re-layouts: 1.08 us -> none  [on_device(): rows = jnp.transpose(fields, (1, 0, 2, 3)).reshape(xc * cin, yc * zc)]
where the time goes in v2:
time: 46.2 us; the launch traced here: 45.4 us
  Pallas kernels  44.6 us (97%)
  local copies, waits for them, and re-layouts  0.8 us (2%)
    pallas_call x1, Pallas kernels, on_device(): pl.pallas_call(functools.partial(kernel, A, B, xc, yc, 1.0 / math.sqrt(ce...  44.6 us

profile of v2, /device:TPU:0, one launch (start us, length us, event | category | flops | bytes accessed | tf_op | source)
XLA Modules:
  0.0 45.4 jit_solution(262162774608748867)
XLA Ops:
  0.0 44.6 %shard_map.199 = f32[4,16,16,128]{3,2,1,0:T(8,128)S(1)} custom-call(f32[4,16,16,128]{3,2,1,0:T(8,128)} %f_hbm.1, f32[4,32]{1,0:T(4,128)} %bitcast.9, f32[1,32]{1,0:T(1,128)} %bitcast.10, f32[32,64]{1,0:T(8,128)} %bitcast.8, f32[1,64]{1,0:T(1,128)} %bitcast.11, f32[32,64]{1,0:T(8,128)} %wo_hbm.1, f32[1,32]{1,0:T(1,128)} %bitcast.12, f32[4,32]{1,0:T(4,128)} %pr_hbm.1, ...), custom_call_target="tpu_custom_call" | custom-call | tf_op jit(solution)/shard_map/pallas_call | solution.py:607
  44.6 0.8 %copy.23 = f32[4,16,16,128]{3,2,1,0:T(8,128)} copy(f32[4,16,16,128]{3,2,1,0:T(8,128)S(1)} %shard_map.199) | data formatting | bytes 1048576

commit v3 on v2

--- a/solution.py
+++ b/solution.py
@@ -103,13 +103,20 @@
     return (0.5 * v) * (1.0 + lax.erf(v * math.sqrt(0.5)))
 
 
+def parts_of(A, H, channels):
+    parts = 1
+    while H % (2 * parts) == 0 and channels % (16 * parts * A) == 0:
+        parts *= 2
+    return parts
+
+
 def kernel(
     A, B, cells_x, cells_y, scale1, scale2, gain,
     f_hbm, lift_hbm, lbias_hbm, byp_hbm, bi_hbm, wo_hbm, bo_hbm, pr_hbm, pb_hbm, tzf_hbm, tzi_hbm, w1_hbm, w2_hbm, tx_hbm, yf1_hbm, yfc_hbm, yic_hbm, yi2_hbm, xf_hbm, xi_hbm, xo_hbm,
     o_ref,
     fx, f_ref, lift_ref, lbias_ref, byp_ref, bi_ref, wo_ref, bo_ref, pr_ref, pb_ref, tzf_ref, os_ref,
     tzi_ref, w1, w2, tx, yf1, yfc, yic, yi2, xf, xi, xo,
-    buf1, r1, mx, mt1, r5, buf5, yall, pg, pk_ref, vx, zc, vn, buf2, r3, buf4, r4, ag2, vf, nar, fk_ref, t16, bd, bpq,
+    buf1, r1, mx, mt1, g1, lines, yall, pg, pk_ref, vx, zc, vn, buf2, r3, ag2, vf, nar, fk_ref, t16, bd, bpq,
     fsem, csem, ssem, rsem,
 ):
     a = lax.axis_index("gx")
@@ -122,13 +129,14 @@
     X = A // 2
     CIN, C1 = lift_ref.shape
     C2 = wo_ref.shape[1]
-    CQ = C2 // A
+    S = parts_of(A, H, C2)
+    CQ = C2 // (A * S)
     CG = CQ // 8
     hx = cells_x // 2
     HX = hx * A
     G1 = GROUP * C2 // CQ
-    own_g = b // H
-    own_h = lax.rem(b, H)
+    part = lax.rem(b, S)
+    base = b - part
     core = lax.rem(a, 2)
     sib = a + 1 - 2 * core
 
@@ -137,7 +145,7 @@
         (tzf_hbm, tzf_ref), (tx_hbm.at[a], tx), (yf1_hbm.at[b], yf1), (lift_hbm, lift_ref), (lbias_hbm, lbias_ref),
         (byp_hbm, byp_ref), (bi_hbm, bi_ref), (wo_hbm, wo_ref), (bo_hbm, bo_ref), (pr_hbm, pr_ref), (pb_hbm, pb_ref),
         (w1_hbm, w1), (xi_hbm, xi), (tzi_hbm, tzi_ref), (xf_hbm, xf), (w2_hbm, w2), (yi2_hbm.at[b], yi2), (xo_hbm.at[a], xo),
-    ] + [(yic_hbm.at[g * H + own_h], yic.at[g]) for g in range(IL)] + [(yfc_hbm.at[g * H + own_h], yfc.at[g]) for g in range(IL)]
+    ] + [(yic_hbm.at[base + n], yic.at[n]) for n in range(S)] + [(yfc_hbm.at[base + n], yfc.at[n]) for n in range(S)]
     loads = [pltpu.make_async_copy(src, dst, csem.at[k]) for k, (src, dst) in enumerate(pairs)]
     l_tzf, l_tx, l_yf1 = loads[:3]
     l_w1, l_xi, l_tzi, l_xf, l_w2, l_yi2, l_xo = loads[11:18]
@@ -180,8 +188,8 @@
     def at(index):
         return (index // B, lax.rem(index, B))
 
-    A2A, PAIR1, EXP1, RED, PAIR2, EXP2, POOL, YALL = range(8)
-    SPREAD = 8
+    A2A, EXP1, RED, EXP2, LINE_PAIR, POOL, POOL_X, POOL_Y, POOL_XY, LINE = range(10)
+    SPREAD = LINE + S
     NEAR = SPREAD + X * B
 
     width = tzi_ref.shape[1]
@@ -200,10 +208,10 @@
     for z in zs:
         us.append(mul3((tx[0], tx[1]), split(jnp.concatenate([z, rot_f(z)], axis=0))))
     l_yf1.wait()
-    part = mul3(split(jnp.concatenate(us, axis=1)), (yf1[0], yf1[1]))
+    parts = mul3(split(jnp.concatenate(us, axis=1)), (yf1[0], yf1[1]))
     for i in range(KX):
         for h in range(H):
-            buf1[i * H + h] = part[i * CIN:(i + 1) * CIN, h * LB:(h + 1) * LB]
+            buf1[i * H + h] = parts[i * CIN:(i + 1) * CIN, h * LB:(h + 1) * LB]
     r1[me] = buf1[me]
     pl.semaphore_wait(barrier, N - 1)
 
@@ -217,26 +225,73 @@
             both[:, 2 * y * zn:(2 * y + 1) * zn] + both[:, (2 * y + 1) * zn:(2 * y + 2) * zn]
             for y in range(YB)
         ]
-        pg[a, x * CIN:(x + 1) * CIN] = jnp.concatenate(pieces, axis=1) * 0.25
+        pg[a * S + part, x * CIN:(x + 1) * CIN] = jnp.concatenate(pieces, axis=1) * 0.25
 
     def near_slot(phase, step):
-        return NEAR + (phase - POOL) * X + step
-
-    def near_send(buffer, phase):
+        return NEAR + (phase - LINE) * X + step
+
+    square = X == 2 and S == 2
+    mate = lax.rem(a + 2, A)
+    other = S - 1 - part
+
+    def share_send(buffer):
+        own = buffer.at[a * S + part]
+        if square:
+            remote(own, own, POOL, POOL_X, (mate, b))
+            remote(own, own, POOL, POOL_Y, (a, base + other))
+            remote(own, own, POOL, POOL, (sib, b))
+        else:
+            for ia in range(A):
+                for turn in range(S):
+                    if ia or turn:
+                        remote(own, own, POOL, POOL, (lax.rem(a + ia, A), base + member(turn)))
+
+    def share_relay(buffer):
+        if square:
+            left = buffer.at[mate * S + part]
+            right = buffer.at[a * S + other]
+            arrive(left, POOL_X)
+            arrive(right, POOL_Y)
+            ia = a * core + mate * (1 - core)
+            ip = other * core + part * (1 - core)
+            target = (mate * core + a * (1 - core), b * core + (base + other) * (1 - core))
+            relayed = buffer.at[ia * S + ip]
+            remote(relayed, relayed, POOL, POOL_XY, target)
+            remote(left, left, POOL, POOL, (sib, b))
+            remote(right, right, POOL, POOL, (sib, b))
+
+    def share_last(buffer):
+        if square:
+            corner = buffer.at[mate * S + other]
+            arrive(corner, POOL_XY)
+            remote(corner, corner, POOL, POOL, (sib, b))
+
+    def share_finish(buffer):
+        arrive(buffer.at[pl.ds(0, A * S // 2 if square else A * S - 1)], POOL)
+
+    def member(turn):
+        return lax.rem(part + turn, S)
+
+    def pair_finish(buffer, phase):
+        if S > 1:
+            arrive(buffer.at[0, pl.ds(0, S - 1)], phase)
+
+    def near_send(buffer, phase, turn):
+        own = buffer.at[a, member(turn)]
         for step in range(1, X):
-            remote(buffer.at[a], buffer.at[a], phase, near_slot(phase, step), (lax.rem(a + 2 * step, A), b))
-        remote(buffer.at[a], buffer.at[a], phase, phase, (sib, b))
-
-    def near_forward(buffer, phase):
+            remote(own, own, phase + turn, near_slot(phase + turn, step), (lax.rem(a + 2 * step, A), b))
+        remote(own, own, phase + turn, phase + turn, (sib, b))
+
+    def near_forward(buffer, phase, turn):
         for step in range(1, X):
-            peer = lax.rem(a + A - 2 * step, A)
-            arrive(buffer.at[peer], near_slot(phase, step))
-            remote(buffer.at[peer], buffer.at[peer], phase, phase, (sib, b))
-
-    def near_finish(buffer, phase):
-        arrive(buffer.at[pl.ds(0, X)], phase)
-
-    near_send(pg, POOL)
+            other = buffer.at[lax.rem(a + A - 2 * step, A), member(turn)]
+            arrive(other, near_slot(phase + turn, step))
+            remote(other, other, phase + turn, phase + turn, (sib, b))
+
+    def near_finish(buffer, phase, turn):
+        arrive(buffer.at[pl.ds(0, X), 0], phase + turn)
+
+    share_send(pg)
 
     for load in loads[3:12]:
         load.wait()
@@ -280,9 +335,9 @@
         return bd[0:count * rows, 0:count * cols]
 
     bp_all = bp16.astype(F32)
-    for q in range(A):
+    for q in range(A * S):
         bpq[q] = bp_all[q * CQ:(q + 1) * CQ]
-    bq_bd = diagonal(bpq[a], G1).astype(BF16)
+    bq_bd = diagonal(bpq[a * S + part], G1).astype(BF16)
     bp_bd = diagonal(bp_all, GROUP).astype(BF16)
     pl_bd = diagonal(pl16.astype(F32), GROUP).astype(BF16)
     wo_bd = wide(split(diagonal(wo_ref[...], GROUP)))
@@ -310,18 +365,12 @@
     first = jnp.where((lane == 0) & (me == 0), gain, 0.0).astype(F32)
     st = st + columns[:, CIN:CIN + 1] * first
     mixed = mix(st, w1, C2)
-    mt1[...] = mixed
-    r5[own_h] = mixed
-
-    def group_member(step):
-        return own_g * H + lax.rem(own_h + step, H)
-
-    def column(ia, ig):
-        return lax.rem(a + ia, A), lax.rem(own_g + ig, IL) * H + own_h
-
-    order = [(ia, ig) for ig in range(IL) for ia in range(A) if ia or ig]
-    for t in range(1, H):
-        remote(mt1, r5.at[own_h], PAIR1, PAIR1, (a, group_member(t)))
+    for q in range(A * S):
+        mt1[q] = mixed[q * CQ:(q + 1) * CQ]
+    g1[me] = mt1[a * S + part]
+    for step in range(1, N):
+        pa, pb = at(lax.rem(me + step, N))
+        remote(mt1.at[pa * S + lax.rem(pb, S)], g1.at[me], EXP1, EXP1, (pa, pb))
 
     def fill(value):
         n = value.shape[1]
@@ -331,30 +380,35 @@
         t16[2 * CIN:3 * CIN, :n] = high.astype(F32)
         return t16[:, :n].astype(BF16)
 
+    def fill_pooled(ia, ip):
+        for x in range(hx):
+            pk_ref[ip * HX + ia * hx + x] = fill(pg[ia * S + ip, x * CIN:(x + 1) * CIN])
+
+    share_relay(pg)
     for x in range(cells_x):
         fk_ref[x] = fill(f_ref[x * CIN:(x + 1) * CIN])
-    near_forward(pg, POOL)
-    for load in loads[18:18 + IL]:
+    if square:
+        fill_pooled(a, part)
+        fill_pooled(mate, part)
+        fill_pooled(a, other)
+        share_last(pg)
+        fill_pooled(mate, other)
+    for load in loads[18:18 + S]:
         load.wait()
-    arrive(r5.at[pl.ds(0, H - 1)], PAIR1)
-    rows = jnp.concatenate([r5[h] for h in range(H)], axis=1)
-    tables = tuple(jnp.concatenate([yic[g, n] for g in range(IL)], axis=1) for n in range(2))
+    arrive(g1.at[pl.ds(0, N - 1)], EXP1)
+    rows = jnp.concatenate(
+        [jnp.concatenate([g1[i * H + h] for h in range(H)], axis=1) for i in range(KX)], axis=0
+    )
+    tables = tuple(jnp.concatenate([yic[n, k] for n in range(S)], axis=1) for k in range(2))
     y = mul3(split(rows), tables)
-    for q in range(A):
-        for g in range(IL):
-            buf5[q * IL + g] = y[q * CQ:(q + 1) * CQ, g * LB:(g + 1) * LB]
-    mine = a * IL + own_g
-    for ia, ig in reversed(order):
-        pa, pb = column(ia, ig)
-        remote(buf5.at[pa * IL + pb // H], yall.at[pa, mine], EXP1, EXP1, (pa, pb))
-    yall[a, mine] = buf5[mine]
-    near_finish(pg, POOL)
-    for q in range(A):
-        for x in range(hx):
-            pk_ref[q * hx + x] = fill(pg[q, x * CIN:(x + 1) * CIN])
-    arrive(yall.at[a, pl.ds(0, KX - 1)], EXP1)
-    near_send(yall, YALL)
-    y = jnp.concatenate([yall[a, i] for i in range(KX)], axis=0)
+    for n in range(S):
+        for i in range(KX):
+            lines[n, i] = y[i * CQ:(i + 1) * CQ, n * LB:(n + 1) * LB]
+    for turn in range(1, S):
+        remote(lines.at[member(turn)], yall.at[a, part], LINE_PAIR, LINE_PAIR, (a, base + member(turn)))
+    for i in range(KX):
+        yall[a, part, i] = lines[part, i]
+    near_send(yall, LINE, 0)
 
     def modes(value, rows_each):
         groups = rows_each // 8
@@ -371,12 +425,17 @@
         jnp.concatenate([xi[q, 0] for q in range(A)], axis=0),
         jnp.concatenate([xi[q, 1] for q in range(A)], axis=0),
     ))
-    v = mul(table, deep(split(jnp.concatenate(modes(y, CQ), axis=1))))
-    for s in range(HX // G1):
-        vx[s] = jnp.concatenate([
-            v[(s * G1 + xx) * 8:(s * G1 + xx) * 8 + 8, g * LB:(g + 1) * LB]
-            for xx in range(G1) for g in range(CG)
-        ], axis=0)
+    halves_y = []
+    for n in range(S):
+        halves_y += modes(y[:, n * LB:(n + 1) * LB], CQ)
+    v = mul(table, deep(split(jnp.concatenate(halves_y, axis=1))))
+    steps = HX // G1
+    for n in range(S):
+        for s in range(steps):
+            vx[n * steps + s] = jnp.concatenate([
+                v[(s * G1 + xx) * 8:(s * G1 + xx) * 8 + 8, (n * CG + g) * LB:(n * CG + g + 1) * LB]
+                for xx in range(G1) for g in range(CG)
+            ], axis=0)
 
     def coarse_step(s, carry):
         v = mul(tall(split(vx[s])), tzi_ref[...])
@@ -385,68 +444,56 @@
         zc[s] = mul(tall(g), tzf_ref[...])
         return carry
 
+    share_finish(pg)
+    for ia in (sib, lax.rem(sib + 2, A)) if square else range(A):
+        for ip in range(S):
+            fill_pooled(ia, ip)
     l_tzi.wait()
-    lax.fori_loop(0, HX // G1, coarse_step, 0)
+    lax.fori_loop(0, S * steps, coarse_step, 0)
 
     l_xf.wait()
+    for load in loads[18 + S:]:
+        load.wait()
     z = jnp.concatenate([
         jnp.concatenate([
-            zc[s, xx * CQ + g * 8:xx * CQ + g * 8 + 8] for s in range(HX // G1) for xx in range(G1)
-        ], axis=0) for g in range(CG)
+            zc[n * steps + s, xx * CQ + g * 8:xx * CQ + g * 8 + 8] for s in range(steps) for xx in range(G1)
+        ], axis=0) for n in range(S) for g in range(CG)
     ], axis=1)
     z = mul(wide((xf[0], xf[1])), deep(split(z)))
-    value = jnp.concatenate([
-        z[i * 8:(i + 1) * 8, g * LB:(g + 1) * LB] for i in range(KX) for g in range(CG)
-    ], axis=0) + rot_f(jnp.concatenate([
-        z[(KX + i) * 8:(KX + i + 1) * 8, g * LB:(g + 1) * LB] for i in range(KX) for g in range(CG)
-    ], axis=0))
+
+    def spectrum(first, n):
+        return jnp.concatenate([
+            z[(first + i) * 8:(first + i + 1) * 8, (n * CG + g) * LB:(n * CG + g + 1) * LB]
+            for i in range(KX) for g in range(CG)
+        ], axis=0)
+
+    value = jnp.concatenate([spectrum(0, n) + rot_f(spectrum(KX, n)) for n in range(S)], axis=1)
+    tables = tuple(jnp.concatenate([yfc[n, k] for n in range(S)], axis=0) for k in range(2))
+    out = mul3(split(value), tables)
     for i in range(KX):
-        buf2[i] = value[i * CQ:(i + 1) * CQ]
-    for ia, ig in reversed(order):
-        pa, pb = column(ia, ig)
-        remote(buf2.at[pa * IL + pb // H], r3.at[a * IL + own_g], RED, RED, (pa, pb))
-    r3[a * IL + own_g] = buf2[a * IL + own_g]
-
-    near_forward(yall, YALL)
-    near_finish(yall, YALL)
-    parts = []
+        for h in range(H):
+            buf2[i * H + h] = out[i * CQ:(i + 1) * CQ, h * LB:(h + 1) * LB]
+    for step in range(1, N):
+        peer = lax.rem(me + step, N)
+        remote(buf2.at[peer], r3.at[me], RED, RED, at(peer))
+    r3[me] = buf2[me]
+
+    pair_finish(yall, LINE_PAIR)
+    for turn in range(1, S):
+        near_send(yall, LINE, turn)
+    near_forward(yall, LINE, 0)
+    l_w2.wait()
+    arrive(r3.at[pl.ds(0, N - 1)], RED)
+    for turn in range(1, S):
+        near_forward(yall, LINE, turn)
+    sums = []
     for q in range(A):
-        parts += modes(jnp.concatenate([yall[q, i] for i in range(KX)], axis=0), CQ)
-    v = mul(wide((xi[a, 0], xi[a, 1])), deep(split(jnp.concatenate(parts, axis=1))))
-    for s in range(hx // GROUP):
-        vn[s] = jnp.concatenate([
-            v[(s * GROUP + xx) * 8:(s * GROUP + xx) * 8 + 8, g * LB:(g + 1) * LB]
-            for xx in range(GROUP) for g in range(C2 // 8)
-        ], axis=0)
-
-    def narrow_step(s, carry):
-        v = mul(tall(split(vn[s])), tzi_ref[...])
-        near = jnp.concatenate([pk_ref[a * hx + s * GROUP + xx] for xx in range(GROUP)], axis=0)
-        g = split(gelu(v + mul(bp_bd, near)))
-        narrow = mul(wo_bd, deep(g))
-        for xx in range(GROUP):
-            nar[s * GROUP + xx] = narrow[xx * C1:(xx + 1) * C1]
-        return carry
-
-    lax.fori_loop(0, hx // GROUP, narrow_step, 0)
-
-    l_w2.wait()
-    for load in loads[18 + IL:]:
-        load.wait()
-    arrive(r3.at[pl.ds(0, KX - 1)], RED)
-    value = jnp.concatenate(
-        [jnp.concatenate([r3[q * IL + g] for g in range(IL)], axis=1) for q in range(A)], axis=0
-    )
-    tables = tuple(jnp.concatenate([yfc[g, n] for g in range(IL)], axis=0) for n in range(2))
-    out = mul3(split(value), tables)
-    for h in range(H):
-        buf4[h] = out[:, h * LB:(h + 1) * LB]
-    for t in range(1, H):
-        peer = lax.rem(own_h + t, H)
-        remote(buf4.at[peer], r4.at[own_h], PAIR2, PAIR2, (a, group_member(t)))
-    r4[own_h] = buf4[own_h]
-    arrive(r4.at[pl.ds(0, H - 1)], PAIR2)
-    st = (jnp.sum(r4[...], axis=0) * scale2).T
+        for n in range(S):
+            total = r3[q * B + n]
+            for t in range(S + n, B, S):
+                total = total + r3[q * B + t]
+            sums.append(total)
+    st = (jnp.concatenate(sums, axis=0) * scale2).T
     mixed = jnp.zeros((C1, LB), F32)
     for j in range(J):
         for k in range(KZ):
@@ -481,6 +528,30 @@
     for t in range(B - 1, 0, -1):
         remote(ag2.at[me], ag2.at[me], EXP2, SPREAD + t, (a, flip(t)))
     spread(0)
+    for turn in range(S):
+        near_finish(yall, LINE, turn)
+    parts = []
+    for q in range(A):
+        for n in range(S):
+            parts += modes(jnp.concatenate([yall[q, n, i] for i in range(KX)], axis=0), CQ)
+    v = mul(wide((xi[a, 0], xi[a, 1])), deep(split(jnp.concatenate(parts, axis=1))))
+    for s in range(hx // GROUP):
+        vn[s] = jnp.concatenate([
+            v[(s * GROUP + xx) * 8:(s * GROUP + xx) * 8 + 8, g * LB:(g + 1) * LB]
+            for xx in range(GROUP) for g in range(C2 // 8)
+        ], axis=0)
+
+    def narrow_step(s, carry):
+        v = mul(tall(split(vn[s])), tzi_ref[...])
+        near = jnp.concatenate([pk_ref[part * HX + a * hx + s * GROUP + xx] for xx in range(GROUP)], axis=0)
+        g = split(gelu(v + mul(bp_bd, near)))
+        narrow = mul(wo_bd, deep(g))
+        for xx in range(GROUP):
+            nar[s * GROUP + xx] = narrow[xx * C1:(xx + 1) * C1]
+        return carry
+
+    lax.fori_loop(0, hx // GROUP, narrow_step, 0)
+
     for t in range(1, B):
         source = a * B + flip(t)
         arrive(ag2.at[source], SPREAD + t)
@@ -533,11 +604,16 @@
         return carry
 
     lax.fori_loop(0, cells_x // GROUP, fine_step, 0)
-    for phase, target in (
-        (A2A, buf1.at[pl.ds(0, N - 1)]), (PAIR1, r5.at[pl.ds(0, H - 1)]), (EXP1, buf5.at[pl.ds(0, KX - 1)]),
-        (RED, buf2.at[pl.ds(0, KX - 1)]), (PAIR2, buf4.at[pl.ds(0, H - 1)]), (EXP2, ag2.at[pl.ds(0, N - 1)]),
-        (POOL, pg.at[pl.ds(0, A - 1)]), (YALL, yall.at[pl.ds(0, A - 1)]),
-    ):
+    waits = [
+        (A2A, buf1.at[pl.ds(0, N - 1)]), (EXP1, g1.at[pl.ds(0, N - 1)]), (RED, buf2.at[pl.ds(0, N - 1)]),
+        (EXP2, ag2.at[pl.ds(0, N - 1)]),
+    ]
+    if S > 1:
+        waits.append((LINE_PAIR, yall.at[0, pl.ds(0, S - 1)]))
+    waits.append((POOL, pg.at[pl.ds(0, A * S - 1)]))
+    for turn in range(S):
+        waits.append((LINE + turn, yall.at[pl.ds(0, A - 1), 0]))
+    for phase, target in waits:
         whole(target, phase, phase).wait_send()
 
 
@@ -555,7 +631,8 @@
     J = KY // H
     N = A * B
     width = YB * zc
-    CQ = C2 // A
+    S = parts_of(A, H, C2)
+    CQ = C2 // (A * S)
     hx = xc // 2
     HX = hx * A
     G1 = GROUP * C2 // CQ
@@ -616,20 +693,20 @@
         ] + [V(v.shape, v.dtype) for v in operands[1:10]] + [
             V((2, YB * GROUP * cin, zc), F32),
             V(tzi.shape, BF16), V(spectral_in.shape, F32), V(weights2.shape, F32),
-            V(tx_t.shape[1:], BF16), V(yf1_t.shape[1:], BF16), V((IL,) + yfc_t.shape[1:], BF16),
-            V((IL,) + yic_t.shape[1:], BF16), V(yi2_t.shape[1:], BF16), V(xf_t.shape, BF16), V(xi_t.shape, BF16),
+            V(tx_t.shape[1:], BF16), V(yf1_t.shape[1:], BF16), V((S,) + yfc_t.shape[1:], BF16),
+            V((S,) + yic_t.shape[1:], BF16), V(yi2_t.shape[1:], BF16), V(xf_t.shape, BF16), V(xi_t.shape, BF16),
             V(xo_t.shape[1:], BF16),
             V((N, cin, LB), F32), V((N, cin, LB), F32), V((LB, LB), F32),
-            V((C2, LB), F32), V((H, C2, LB), F32), V((KX, CQ, LB), F32), V((A, KX, CQ, LB), F32),
-            V((A, hx * cin, width), F32), V((hx * A, 16, width), BF16),
-            V((HX // G1, G1 * CQ, LB), F32), V((HX // G1, G1 * CQ, LB), F32), V((hx // GROUP, GROUP * C2, LB), F32),
-            V((KX, CQ, LB), F32), V((KX, CQ, LB), F32), V((H, C2, LB), F32), V((H, C2, LB), F32), V((N, C1, LB), F32),
+            V((A * S, CQ, LB), F32), V((N, CQ, LB), F32), V((S, KX, CQ, LB), F32), V((A, S, KX, CQ, LB), F32),
+            V((A * S, hx * cin, width), F32), V((S * HX, 16, width), BF16),
+            V((S * HX // G1, G1 * CQ, LB), F32), V((S * HX // G1, G1 * CQ, LB), F32), V((hx // GROUP, GROUP * C2, LB), F32),
+            V((N, CQ, LB), F32), V((N, CQ, LB), F32), V((N, C1, LB), F32),
             V((xc // GROUP, 2, GROUP * C1, LB), F32),
             V((hx, C1, width), F32), V((xc, 16, yc * zc), BF16), V((16, yc * zc), F32),
-            V((GROUP * C2, max(GROUP * C2, G1 * 16)), F32), V((A, CQ, 16), F32),
+            V((GROUP * C2, max(GROUP * C2, G1 * 16)), F32), V((A * S, CQ, 16), F32),
             pltpu.SemaphoreType.DMA((cin,)),
-            pltpu.SemaphoreType.DMA((18 + 2 * IL,)),
-            pltpu.SemaphoreType.DMA((8,)), pltpu.SemaphoreType.DMA((8 + A * B // 2 + A,)),
+            pltpu.SemaphoreType.DMA((18 + 2 * S,)),
+            pltpu.SemaphoreType.DMA((9 + S,)), pltpu.SemaphoreType.DMA((9 + S + A * B // 2 + A * S // 2,)),
         ],
         compiler_params=pltpu.CompilerParams(
             collective_id=0, has_side_effects=True, vmem_limit_bytes=60 * 1024 * 1024

time: 46.2 us -> 43.1 us (0.933)
  Pallas kernels: 44.6 us -> 41.5 us
    pallas_call x1, Pallas kernels: 44.6 us -> 41.5 us  [on_device(): pl.pallas_call(functools.partial(kernel, A, B, xc, yc, 1.0 / math.sqrt(ce...]
where the time goes in v3:
time: 43.1 us; the launch traced here: 42.3 us
  Pallas kernels  41.5 us (96%)
  local copies, waits for them, and re-layouts  0.8 us (2%)
    pallas_call x1, Pallas kernels, on_device(): pl.pallas_call(functools.partial(kernel, A, B, xc, yc, 1.0 / math.sqrt(ce...  41.5 us

profile of v3, /device:TPU:0, one launch (start us, length us, event | category | flops | bytes accessed | tf_op | source)
XLA Modules:
  0.0 42.3 jit_solution(14239500058954832940)
XLA Ops:
  0.0 41.5 %shard_map.199 = f32[4,16,16,128]{3,2,1,0:T(8,128)S(1)} custom-call(f32[4,16,16,128]{3,2,1,0:T(8,128)} %f_hbm.1, f32[4,32]{1,0:T(4,128)} %bitcast.9, f32[1,32]{1,0:T(1,128)} %bitcast.10, f32[32,64]{1,0:T(8,128)} %bitcast.8, f32[1,64]{1,0:T(1,128)} %bitcast.11, f32[32,64]{1,0:T(8,128)} %wo_hbm.1, f32[1,32]{1,0:T(1,128)} %bitcast.12, f32[4,32]{1,0:T(4,128)} %pr_hbm.1, ...), custom_call_target="tpu_custom_call" | custom-call | tf_op jit(solution)/shard_map/pallas_call | solution.py:684
  41.5 0.8 %copy.23 = f32[4,16,16,128]{3,2,1,0:T(8,128)} copy(f32[4,16,16,128]{3,2,1,0:T(8,128)S(1)} %shard_map.199) | data formatting | bytes 1048576

commit v4 on v3

--- a/solution.py
+++ b/solution.py
@@ -15,6 +15,7 @@
 YB = 8
 LB = 128
 GROUP = 4
+FINE = 8
 F32 = jnp.float32
 BF16 = jnp.bfloat16
 MESH = pl.DeviceIdType.MESH
@@ -99,6 +100,16 @@
     return mul(a[0], b[0]) + (mul(a[1], b[0]) + mul(a[0], b[1]))
 
 
+def wide_rows(a):
+    return jnp.concatenate([a[0], a[0], a[1]], axis=0)
+
+
+def left3(table, b):
+    rows = table[0].shape[0]
+    both = mul(jnp.concatenate([table[0], table[1]], axis=0), b[0])
+    return both[:rows] + (both[rows:] + mul(table[0], b[1]))
+
+
 def gelu(v):
     return (0.5 * v) * (1.0 + lax.erf(v * math.sqrt(0.5)))
 
@@ -116,7 +127,7 @@
     o_ref,
     fx, f_ref, lift_ref, lbias_ref, byp_ref, bi_ref, wo_ref, bo_ref, pr_ref, pb_ref, tzf_ref, os_ref,
     tzi_ref, w1, w2, tx, yf1, yfc, yic, yi2, xf, xi, xo,
-    buf1, r1, mx, mt1, g1, lines, yall, pg, pk_ref, vx, zc, vn, buf2, r3, ag2, vf, nar, fk_ref, t16, bd, bpq,
+    buf1, r1, mx, mt1, g1, lines, yall, pg, pk_ref, lw, ones, vx, zc, vn, buf2, r3, ag2, vf, nar, fk_ref, t16, bd, bpq,
     fsem, csem, ssem, rsem,
 ):
     a = lax.axis_index("gx")
@@ -200,9 +211,12 @@
     for y in range(cells_y):
         f_ref[:, y * zn:(y + 1) * zn] = flat[pl.ds(y, f_ref.shape[0], stride=cells_y), :]
     l_tzf.wait()
-    zs = []
-    for ch in range(2):
-        zs.append(mul(tall(split(f_ref[:, ch * width:(ch + 1) * width])), tzf_ref[...]))
+    def wave(pair):
+        both = mul(pair[0], tzf_ref[...])
+        return both[:, :LB] + (both[:, LB:] + mul(pair[1], tzf_ref[:, :LB]))
+
+    zs = wave(split(jnp.concatenate([f_ref[:, :width], f_ref[:, width:]], axis=0)))
+    zs = [zs[:zs.shape[0] // 2], zs[zs.shape[0] // 2:]]
     l_tx.wait()
     us = []
     for z in zs:
@@ -319,6 +333,7 @@
         return mx[...].T[:n, :16].astype(BF16)
 
     highest = lax.Precision.HIGHEST
+    eighth = lax.broadcasted_iota(jnp.int32, (1, ones.shape[1]), 1) // 8
     m = jnp.dot(lift8, byp_ref[...], precision=highest, preferred_element_type=F32)
     bp16 = left16(m, m[CIN:CIN + 1] + bi_ref[...])
     m = lax.dot_general(
@@ -337,34 +352,37 @@
     bp_all = bp16.astype(F32)
     for q in range(A * S):
         bpq[q] = bp_all[q * CQ:(q + 1) * CQ]
-    bq_bd = diagonal(bpq[a * S + part], G1).astype(BF16)
+    bq_bd = diagonal(bpq[a * S + part], min(G1, 16)).astype(BF16)
     bp_bd = diagonal(bp_all, GROUP).astype(BF16)
-    pl_bd = diagonal(pl16.astype(F32), GROUP).astype(BF16)
+    pl_bd = diagonal(pl16.astype(F32), FINE).astype(BF16)
     wo_bd = wide(split(diagonal(wo_ref[...], GROUP)))
-    pr_bd = wide(split(diagonal(pr_ref[...], GROUP)))
+    pr_bd = split(diagonal(pr_ref[...], FINE))
+    Q = J * KZ
+    lifts = tall(split(lift8))
+    for j in range(J):
+        for k in range(KZ):
+            both = []
+            for n in range(2):
+                both.append(mul(lifts, wide_rows(split(w1[j, n, k]))))
+            lw[0, j * KZ + k] = jnp.concatenate([both[0], both[1]], axis=1)
+            lw[1, j * KZ + k] = jnp.concatenate([-both[1], both[0]], axis=1)
+    for row in range(Q):
+        ones[row:row + 1] = jnp.where(eighth == row, 1.0, 0.0).astype(F32)
+    blocks = ones[...].astype(BF16)
     arrive(r1.at[pl.ds(0, N - 1)], A2A)
 
-    def mix(st, w, width_out):
-        mx[...] = jnp.zeros_like(mx)
-        for j in range(J):
-            for k in range(KZ):
-                q = j * KZ + k
-                p = J * KZ + q
-                re = st[:, q:q + 1]
-                im = st[:, p:p + 1]
-                wr = w[j, 0, k]
-                wi = w[j, 1, k]
-                mx[q:q + 1, :width_out] = jnp.sum(re * wr - im * wi, axis=0, keepdims=True)
-                mx[p:p + 1, :width_out] = jnp.sum(re * wi + im * wr, axis=0, keepdims=True)
-        return mx[...].T[:width_out]
-
     s4 = jnp.sum(r1[...], axis=0) * scale1
-    st = columns[:, 0:1] * s4[0:1]
-    for c in range(1, CIN):
-        st = st + columns[:, c:c + 1] * s4[c:c + 1]
     first = jnp.where((lane == 0) & (me == 0), gain, 0.0).astype(F32)
-    st = st + columns[:, CIN:CIN + 1] * first
-    mixed = mix(st, w1, C2)
+    mx[...] = jnp.zeros_like(mx)
+    mx[0:CIN] = s4
+    mx[CIN:CIN + 1] = first
+    s8 = mx[0:8]
+    mixed = split(jnp.concatenate(
+        [s8[:, q:q + 1] * lw[0, q] + s8[:, Q + q:Q + q + 1] * lw[1, q] for q in range(Q)], axis=0
+    ))
+    mx[0:Q] = mul(blocks, mixed[0]) + mul(blocks, mixed[1])
+    turned = mx[...].T
+    mixed = turned[:C2] + pltpu.roll(turned[C2:], Q, 1)
     for q in range(A * S):
         mt1[q] = mixed[q * CQ:(q + 1) * CQ]
     g1[me] = mt1[a * S + part]
@@ -421,14 +439,11 @@
         return parts
 
     l_xi.wait()
-    table = wide((
-        jnp.concatenate([xi[q, 0] for q in range(A)], axis=0),
-        jnp.concatenate([xi[q, 1] for q in range(A)], axis=0),
-    ))
+    table = tuple(jnp.concatenate([xi[q, k] for q in range(A)], axis=0) for k in range(2))
     halves_y = []
     for n in range(S):
         halves_y += modes(y[:, n * LB:(n + 1) * LB], CQ)
-    v = mul(table, deep(split(jnp.concatenate(halves_y, axis=1))))
+    v = left3(table, split(jnp.concatenate(halves_y, axis=1)))
     steps = HX // G1
     for n in range(S):
         for s in range(steps):
@@ -439,9 +454,13 @@
 
     def coarse_step(s, carry):
         v = mul(tall(split(vx[s])), tzi_ref[...])
-        near = jnp.concatenate([pk_ref[s * G1 + xx] for xx in range(G1)], axis=0)
-        g = split(gelu(v + mul(bq_bd, near)))
-        zc[s] = mul(tall(g), tzf_ref[...])
+        count = min(G1, 16)
+        near = jnp.concatenate([
+            mul(bq_bd, jnp.concatenate([pk_ref[s * G1 + g + xx] for xx in range(count)], axis=0))
+            for g in range(0, G1, count)
+        ], axis=0)
+        g = split(gelu(v + near))
+        zc[s] = wave(g)
         return carry
 
     share_finish(pg)
@@ -498,14 +517,13 @@
     for j in range(J):
         for k in range(KZ):
             q = j * KZ + k
-            p = J * KZ + q
             re = st[q:q + 1]
-            im = st[p:p + 1]
+            im = st[Q + q:Q + q + 1]
             wr = w2[j, 0, k]
             wi = w2[j, 1, k]
             real = jnp.sum(re * wr - im * wi, axis=1, keepdims=True)
             imag = jnp.sum(re * wi + im * wr, axis=1, keepdims=True)
-            mixed = jnp.where(lane == q, real, jnp.where(lane == p, imag, mixed))
+            mixed = jnp.where(lane == q, real, jnp.where(lane == Q + q, imag, mixed))
     ag2[me] = mixed
 
     def flip(t):
@@ -517,12 +535,16 @@
             bit *= 2
         return value
 
+    NEARBY = B // 2
+
     def spread(t):
         source = a * B + flip(t)
         for step in range(1, X):
             remote(
                 ag2.at[source], ag2.at[source], EXP2, SPREAD + step * B + t, (lax.rem(a + 2 * step, A), b)
             )
+            if t >= NEARBY:
+                remote(ag2.at[source], ag2.at[source], EXP2, EXP2, (lax.rem(sib + 2 * step, A), b))
         remote(ag2.at[source], ag2.at[source], EXP2, EXP2, (sib, b))
 
     for t in range(B - 1, 0, -1):
@@ -534,7 +556,7 @@
     for q in range(A):
         for n in range(S):
             parts += modes(jnp.concatenate([yall[q, n, i] for i in range(KX)], axis=0), CQ)
-    v = mul(wide((xi[a, 0], xi[a, 1])), deep(split(jnp.concatenate(parts, axis=1))))
+    v = left3((xi[a, 0], xi[a, 1]), split(jnp.concatenate(parts, axis=1)))
     for s in range(hx // GROUP):
         vn[s] = jnp.concatenate([
             v[(s * GROUP + xx) * 8:(s * GROUP + xx) * 8 + 8, g * LB:(g + 1) * LB]
@@ -560,7 +582,8 @@
         for step in range(1, X):
             source = lax.rem(a + A - 2 * step, A) * B + flip(t)
             arrive(ag2.at[source], SPREAD + step * B + t)
-            remote(ag2.at[source], ag2.at[source], EXP2, EXP2, (sib, b))
+            if t < NEARBY:
+                remote(ag2.at[source], ag2.at[source], EXP2, EXP2, (sib, b))
     arrive(ag2.at[pl.ds(0, X * B)], EXP2)
 
     l_yi2.wait()
@@ -570,22 +593,22 @@
     )
     y = mul3(split(rows), (yi2[0], yi2[1]))
     halves_y = [modes(y[:, ch * LB:(ch + 1) * LB], C1) for ch in range(2)]
-    v = mul(wide((xo[0], xo[1])), deep(split(jnp.concatenate(halves_y[0] + halves_y[1], axis=1))))
+    v = left3((xo[0], xo[1]), split(jnp.concatenate(halves_y[0] + halves_y[1], axis=1)))
     CF = C1 // 8
-    for s in range(cells_x // GROUP):
+    for s in range(cells_x // FINE):
         for ch in range(2):
             vf[s, ch] = jnp.concatenate([
-                v[(s * GROUP + xx) * 8:(s * GROUP + xx) * 8 + 8, (ch * CF + g) * LB:(ch * CF + g + 1) * LB]
-                for xx in range(GROUP) for g in range(CF)
+                v[(s * FINE + xx) * 8:(s * FINE + xx) * 8 + 8, (ch * CF + g) * LB:(ch * CF + g + 1) * LB]
+                for xx in range(FINE) for g in range(CF)
             ], axis=0)
 
     def fine_step(group, carry):
-        near = jnp.concatenate([fk_ref[group * GROUP + xx] for xx in range(GROUP)], axis=0)
+        near = jnp.concatenate([fk_ref[group * FINE + xx] for xx in range(FINE)], axis=0)
         for ch in range(2):
             v = mul(tall(split(vf[group, ch])), tzi_ref[...])
             rows = []
-            for xx in range(0, GROUP, 2):
-                half = nar.at[group * (GROUP // 2) + xx // 2]
+            for xx in range(0, FINE, 2):
+                half = nar.at[group * (FINE // 2) + xx // 2]
                 pieces = []
                 for yy in range(YB):
                     at_y = (ch * YB + yy) // 2 * zn
@@ -593,17 +616,17 @@
                 rows += [jnp.concatenate(pieces, axis=1) + bo_col] * 2
             g = split(gelu(v + jnp.concatenate(rows, axis=0)))
             cols = slice(ch * width, (ch + 1) * width)
-            res = mul(pr_bd, deep(g)) + mul(pl_bd, near[:, cols])
+            res = left3(pr_bd, g) + mul(pl_bd, near[:, cols])
             for yy in range(YB):
-                os_ref[ch, yy * GROUP * CIN:(yy + 1) * GROUP * CIN] = res[:, yy * zn:(yy + 1) * zn]
-            for xx in range(GROUP):
+                os_ref[ch, yy * FINE * CIN:(yy + 1) * FINE * CIN] = res[:, yy * zn:(yy + 1) * zn]
+            for xx in range(FINE):
                 for c in range(CIN):
-                    o_ref[c, group * GROUP + xx, ch * YB:(ch + 1) * YB] = os_ref[
-                        ch, pl.ds(xx * CIN + c, YB, stride=GROUP * CIN), :
+                    o_ref[c, group * FINE + xx, ch * YB:(ch + 1) * YB] = os_ref[
+                        ch, pl.ds(xx * CIN + c, YB, stride=FINE * CIN), :
                     ]
         return carry
 
-    lax.fori_loop(0, cells_x // GROUP, fine_step, 0)
+    lax.fori_loop(0, cells_x // FINE, fine_step, 0, unroll=True)
     waits = [
         (A2A, buf1.at[pl.ds(0, N - 1)]), (EXP1, g1.at[pl.ds(0, N - 1)]), (RED, buf2.at[pl.ds(0, N - 1)]),
         (EXP2, ag2.at[pl.ds(0, N - 1)]),
@@ -640,7 +663,7 @@
     back = math.sqrt(2.0 / (KX * KY * KZ))
 
     tz = z_table(zc)
-    tzf = stacked(tz)
+    tzf = np.concatenate(list(halves(tz)), axis=1)
     tzi = stacked(np.ascontiguousarray(tz.T) * back)
     fine_x = x_angles(A, xc, NX)
     half_x = x_angles(A, xc // 2, NX // 2)
@@ -691,7 +714,7 @@
         scratch_shapes=[
             V((xc, cin, yc, zc), F32), V((xc * cin, yc * zc), F32),
         ] + [V(v.shape, v.dtype) for v in operands[1:10]] + [
-            V((2, YB * GROUP * cin, zc), F32),
+            V((2, YB * FINE * cin, zc), F32),
             V(tzi.shape, BF16), V(spectral_in.shape, F32), V(weights2.shape, F32),
             V(tx_t.shape[1:], BF16), V(yf1_t.shape[1:], BF16), V((S,) + yfc_t.shape[1:], BF16),
             V((S,) + yic_t.shape[1:], BF16), V(yi2_t.shape[1:], BF16), V(xf_t.shape, BF16), V(xi_t.shape, BF16),
@@ -699,11 +722,12 @@
             V((N, cin, LB), F32), V((N, cin, LB), F32), V((LB, LB), F32),
             V((A * S, CQ, LB), F32), V((N, CQ, LB), F32), V((S, KX, CQ, LB), F32), V((A, S, KX, CQ, LB), F32),
             V((A * S, hx * cin, width), F32), V((S * HX, 16, width), BF16),
+            V((2, J * KZ, 8, 2 * C2), F32), V((J * KZ, J * KZ * 8), F32),
             V((S * HX // G1, G1 * CQ, LB), F32), V((S * HX // G1, G1 * CQ, LB), F32), V((hx // GROUP, GROUP * C2, LB), F32),
             V((N, CQ, LB), F32), V((N, CQ, LB), F32), V((N, C1, LB), F32),
-            V((xc // GROUP, 2, GROUP * C1, LB), F32),
+            V((xc // FINE, 2, FINE * C1, LB), F32),
             V((hx, C1, width), F32), V((xc, 16, yc * zc), BF16), V((16, yc * zc), F32),
-            V((GROUP * C2, max(GROUP * C2, G1 * 16)), F32), V((A * S, CQ, 16), F32),
+            V((GROUP * C2, GROUP * C2), F32), V((A * S, CQ, 16), F32),
             pltpu.SemaphoreType.DMA((cin,)),
             pltpu.SemaphoreType.DMA((18 + 2 * S,)),
             pltpu.SemaphoreType.DMA((9 + S,)), pltpu.SemaphoreType.DMA((9 + S + A * B // 2 + A * S // 2,)),

time: 43.1 us -> 41.2 us (0.956); the launches traced: 42.3 us -> 41.1 us
  Pallas kernels: 41.5 us -> 40.2 us
    pallas_call x1, Pallas kernels: 41.5 us -> 40.2 us  [on_device(): pl.pallas_call(functools.partial(kernel, A, B, xc, yc, 1.0 / math.sqrt(ce...]
where the time goes in v4:
time: 41.2 us; the launch traced here: 41.1 us
  Pallas kernels  40.2 us (98%)
  local copies, waits for them, and re-layouts  0.8 us (2%)
    pallas_call x1, Pallas kernels, on_device(): pl.pallas_call(functools.partial(kernel, A, B, xc, yc, 1.0 / math.sqrt(ce...  40.2 us

profile of v4, /device:TPU:0, one launch (start us, length us, event | category | flops | bytes accessed | tf_op | source)
XLA Modules:
  0.0 41.1 jit_solution(8636094401446795553)
XLA Ops:
  0.0 40.2 %shard_map.199 = f32[4,16,16,128]{3,2,1,0:T(8,128)S(1)} custom-call(f32[4,16,16,128]{3,2,1,0:T(8,128)} %f_hbm.1, f32[4,32]{1,0:T(4,128)} %bitcast.9, f32[1,32]{1,0:T(1,128)} %bitcast.10, f32[32,64]{1,0:T(8,128)} %bitcast.8, f32[1,64]{1,0:T(1,128)} %bitcast.11, f32[32,64]{1,0:T(8,128)} %wo_hbm.1, f32[1,32]{1,0:T(1,128)} %bitcast.12, f32[4,32]{1,0:T(4,128)} %pr_hbm.1, ...), custom_call_target="tpu_custom_call" | custom-call | tf_op jit(solution)/shard_map/pallas_call | solution.py:707
  40.3 0.8 %copy.23 = f32[4,16,16,128]{3,2,1,0:T(8,128)} copy(f32[4,16,16,128]{3,2,1,0:T(8,128)S(1)} %shard_map.199) | data formatting | bytes 1048576

commit v5 on v4

--- a/solution.py
+++ b/solution.py
@@ -127,7 +127,7 @@
     o_ref,
     fx, f_ref, lift_ref, lbias_ref, byp_ref, bi_ref, wo_ref, bo_ref, pr_ref, pb_ref, tzf_ref, os_ref,
     tzi_ref, w1, w2, tx, yf1, yfc, yic, yi2, xf, xi, xo,
-    buf1, r1, mx, mt1, g1, lines, yall, pg, pk_ref, lw, ones, vx, zc, vn, buf2, r3, ag2, vf, nar, fk_ref, t16, bd, bpq,
+    buf1, r1, mx, mt1, g1, lines, yall, pg, pk_ref, lw, ones, ye, vx, zc, vn, buf2, r3, ag2, vf, nar, fk_ref, t16, bd, bpq,
     fsem, csem, ssem, rsem,
 ):
     a = lax.axis_index("gx")
@@ -151,6 +151,19 @@
     core = lax.rem(a, 2)
     sib = a + 1 - 2 * core
 
+    def flip(t):
+        value = b
+        bit = 1
+        while bit < B:
+            if t & bit:
+                value = value + bit - 2 * bit * lax.rem(b // bit, 2)
+            bit *= 2
+        return value
+
+    lines_b = [flip(t) for t in range(B)]
+    lines_a = [lax.rem(a + ia, A) for ia in range(A)]
+    peers = [(lines_a[ia], lines_b[t]) for t in reversed(range(B)) for ia in reversed(range(A)) if t or ia]
+
     fields = [pltpu.make_async_copy(f_hbm.at[c], fx.at[:, c], fsem.at[c]) for c in range(CIN)]
     pairs = [
         (tzf_hbm, tzf_ref), (tx_hbm.at[a], tx), (yf1_hbm.at[b], yf1), (lift_hbm, lift_ref), (lbias_hbm, lbias_ref),
@@ -164,11 +177,8 @@
         load.start()
 
     barrier = pltpu.get_barrier_semaphore()
-    for step in range(1, N):
-        peer = lax.rem(me + step, N)
-        pl.semaphore_signal(
-            barrier, inc=1, device_id=(peer // B, lax.rem(peer, B)), device_id_type=MESH
-        )
+    for pa, pb in peers:
+        pl.semaphore_signal(barrier, inc=1, device_id=(pa, pb), device_id_type=MESH)
     for load in loads[3:]:
         load.start()
 
@@ -196,10 +206,7 @@
     def arrive(target, slot):
         whole(target, 0, slot).wait_recv()
 
-    def at(index):
-        return (index // B, lax.rem(index, B))
-
-    A2A, EXP1, RED, EXP2, LINE_PAIR, POOL, POOL_X, POOL_Y, POOL_XY, LINE = range(10)
+    A2A, EXP1, RED, EXP2, LINE_PAIR, POOL, POOL_X, POOL_Y, POOL_XY, POOL_LAST, LINE = range(11)
     SPREAD = LINE + S
     NEAR = SPREAD + X * B
 
@@ -229,9 +236,8 @@
     r1[me] = buf1[me]
     pl.semaphore_wait(barrier, N - 1)
 
-    for step in range(1, N):
-        peer = lax.rem(me + step, N)
-        remote(buf1.at[peer], r1.at[me], A2A, A2A, at(peer))
+    for pa, pb in peers:
+        remote(buf1.at[pa * B + pb], r1.at[me], A2A, A2A, (pa, pb))
 
     for x in range(hx):
         both = f_ref[2 * x * CIN:(2 * x + 1) * CIN] + f_ref[(2 * x + 1) * CIN:(2 * x + 2) * CIN]
@@ -278,10 +284,10 @@
         if square:
             corner = buffer.at[mate * S + other]
             arrive(corner, POOL_XY)
-            remote(corner, corner, POOL, POOL, (sib, b))
+            remote(corner, corner, POOL, POOL_LAST, (sib, b))
 
     def share_finish(buffer):
-        arrive(buffer.at[pl.ds(0, A * S // 2 if square else A * S - 1)], POOL)
+        arrive(buffer.at[pl.ds(0, A * S // 2 - 1 if square else A * S - 1)], POOL)
 
     def member(turn):
         return lax.rem(part + turn, S)
@@ -386,8 +392,7 @@
     for q in range(A * S):
         mt1[q] = mixed[q * CQ:(q + 1) * CQ]
     g1[me] = mt1[a * S + part]
-    for step in range(1, N):
-        pa, pb = at(lax.rem(me + step, N))
+    for pa, pb in peers:
         remote(mt1.at[pa * S + lax.rem(pb, S)], g1.at[me], EXP1, EXP1, (pa, pb))
 
     def fill(value):
@@ -409,6 +414,10 @@
         fill_pooled(a, part)
         fill_pooled(mate, part)
         fill_pooled(a, other)
+        share_finish(pg)
+        fill_pooled(sib, part)
+        fill_pooled(lax.rem(sib + 2, A), part)
+        fill_pooled(sib, other)
         share_last(pg)
         fill_pooled(mate, other)
     for load in loads[18:18 + S]:
@@ -463,10 +472,14 @@
         zc[s] = wave(g)
         return carry
 
-    share_finish(pg)
-    for ia in (sib, lax.rem(sib + 2, A)) if square else range(A):
-        for ip in range(S):
-            fill_pooled(ia, ip)
+    if square:
+        arrive(pg.at[lax.rem(sib + 2, A) * S + other], POOL_LAST)
+        fill_pooled(lax.rem(sib + 2, A), other)
+    else:
+        share_finish(pg)
+        for ia in range(A):
+            for ip in range(S):
+                fill_pooled(ia, ip)
     l_tzi.wait()
     lax.fori_loop(0, S * steps, coarse_step, 0)
 
@@ -492,9 +505,8 @@
     for i in range(KX):
         for h in range(H):
             buf2[i * H + h] = out[i * CQ:(i + 1) * CQ, h * LB:(h + 1) * LB]
-    for step in range(1, N):
-        peer = lax.rem(me + step, N)
-        remote(buf2.at[peer], r3.at[me], RED, RED, at(peer))
+    for pa, pb in peers:
+        remote(buf2.at[pa * B + pb], r3.at[me], RED, RED, (pa, pb))
     r3[me] = buf2[me]
 
     pair_finish(yall, LINE_PAIR)
@@ -526,15 +538,6 @@
             mixed = jnp.where(lane == q, real, jnp.where(lane == Q + q, imag, mixed))
     ag2[me] = mixed
 
-    def flip(t):
-        value = b
-        bit = 1
-        while bit < B:
-            if t & bit:
-                value = value + bit - 2 * bit * lax.rem(b // bit, 2)
-            bit *= 2
-        return value
-
     NEARBY = B // 2
 
     def spread(t):
@@ -578,20 +581,28 @@
         source = a * B + flip(t)
         arrive(ag2.at[source], SPREAD + t)
         spread(t)
+    def expand(ia):
+        rows = jnp.concatenate([
+            jnp.concatenate([ag2[(ia * IL + g) * H + h] for h in range(H)], axis=1) for g in range(IL)
+        ], axis=0)
+        ye[ia] = mul3(split(rows), (yi2[0], yi2[1]))
+
+    l_yi2.wait()
+    expand(a)
     for t in range(B):
         for step in range(1, X):
             source = lax.rem(a + A - 2 * step, A) * B + flip(t)
             arrive(ag2.at[source], SPREAD + step * B + t)
             if t < NEARBY:
                 remote(ag2.at[source], ag2.at[source], EXP2, EXP2, (sib, b))
+    for step in range(1, X):
+        expand(lax.rem(a + 2 * step, A))
     arrive(ag2.at[pl.ds(0, X * B)], EXP2)
 
-    l_yi2.wait()
+    for ia in [sib] + [lax.rem(sib + 2 * step, A) for step in range(1, X)]:
+        expand(ia)
     l_xo.wait()
-    rows = jnp.concatenate(
-        [jnp.concatenate([ag2[i * H + h] for h in range(H)], axis=1) for i in range(KX)], axis=0
-    )
-    y = mul3(split(rows), (yi2[0], yi2[1]))
+    y = jnp.concatenate([ye[ia] for ia in range(A)], axis=0)
     halves_y = [modes(y[:, ch * LB:(ch + 1) * LB], C1) for ch in range(2)]
     v = left3((xo[0], xo[1]), split(jnp.concatenate(halves_y[0] + halves_y[1], axis=1)))
     CF = C1 // 8
@@ -722,7 +733,7 @@
             V((N, cin, LB), F32), V((N, cin, LB), F32), V((LB, LB), F32),
             V((A * S, CQ, LB), F32), V((N, CQ, LB), F32), V((S, KX, CQ, LB), F32), V((A, S, KX, CQ, LB), F32),
             V((A * S, hx * cin, width), F32), V((S * HX, 16, width), BF16),
-            V((2, J * KZ, 8, 2 * C2), F32), V((J * KZ, J * KZ * 8), F32),
+            V((2, J * KZ, 8, 2 * C2), F32), V((J * KZ, J * KZ * 8), F32), V((A, IL * C1, 2 * LB), F32),
             V((S * HX // G1, G1 * CQ, LB), F32), V((S * HX // G1, G1 * CQ, LB), F32), V((hx // GROUP, GROUP * C2, LB), F32),
             V((N, CQ, LB), F32), V((N, CQ, LB), F32), V((N, C1, LB), F32),
             V((xc // FINE, 2, FINE * C1, LB), F32),
@@ -730,7 +741,7 @@
             V((GROUP * C2, GROUP * C2), F32), V((A * S, CQ, 16), F32),
             pltpu.SemaphoreType.DMA((cin,)),
             pltpu.SemaphoreType.DMA((18 + 2 * S,)),
-            pltpu.SemaphoreType.DMA((9 + S,)), pltpu.SemaphoreType.DMA((9 + S + A * B // 2 + A * S // 2,)),
+            pltpu.SemaphoreType.DMA((10 + S,)), pltpu.SemaphoreType.DMA((10 + S + A * B // 2 + A * S // 2,)),
         ],
         compiler_params=pltpu.CompilerParams(
             collective_id=0, has_side_effects=True, vmem_limit_bytes=60 * 1024 * 1024

time: 41.2 us -> 40.5 us (0.983)
  Pallas kernels: 40.2 us -> 39.6 us
    pallas_call x1, Pallas kernels: 40.2 us -> 39.6 us  [on_device(): pl.pallas_call(functools.partial(kernel, A, B, xc, yc, 1.0 / math.sqrt(ce...]
where the time goes in v5:
time: 40.5 us; the launch traced here: 40.4 us
  Pallas kernels  39.6 us (98%)
  local copies, waits for them, and re-layouts  0.8 us (2%)
    pallas_call x1, Pallas kernels, on_device(): pl.pallas_call(functools.partial(kernel, A, B, xc, yc, 1.0 / math.sqrt(ce...  39.6 us

profile of v5, /device:TPU:0, one launch (start us, length us, event | category | flops | bytes accessed | tf_op | source)
XLA Modules:
  0.0 40.4 jit_solution(5471599046659867608)
XLA Ops:
  0.0 39.6 %shard_map.199 = f32[4,16,16,128]{3,2,1,0:T(8,128)S(1)} custom-call(f32[4,16,16,128]{3,2,1,0:T(8,128)} %f_hbm.1, f32[4,32]{1,0:T(4,128)} %bitcast.9, f32[1,32]{1,0:T(1,128)} %bitcast.10, f32[32,64]{1,0:T(8,128)} %bitcast.8, f32[1,64]{1,0:T(1,128)} %bitcast.11, f32[32,64]{1,0:T(8,128)} %wo_hbm.1, f32[1,32]{1,0:T(1,128)} %bitcast.12, f32[4,32]{1,0:T(4,128)} %pr_hbm.1, ...), custom_call_target="tpu_custom_call" | custom-call | tf_op jit(solution)/shard_map/pallas_call | solution.py:718
  39.6 0.8 %copy.23 = f32[4,16,16,128]{3,2,1,0:T(8,128)} copy(f32[4,16,16,128]{3,2,1,0:T(8,128)S(1)} %shard_map.199) | data formatting | bytes 1048576

commit v6 on v5

--- a/solution.py
+++ b/solution.py
@@ -15,10 +15,11 @@
 YB = 8
 LB = 128
 GROUP = 4
-FINE = 8
+FINE = 16
 F32 = jnp.float32
 BF16 = jnp.bfloat16
 MESH = pl.DeviceIdType.MESH
+ROOT = math.sqrt(0.5)
 
 
 def freq(count):
@@ -110,8 +111,8 @@
     return both[:rows] + (both[rows:] + mul(table[0], b[1]))
 
 
-def gelu(v):
-    return (0.5 * v) * (1.0 + lax.erf(v * math.sqrt(0.5)))
+def bend(v):
+    return v * (1.0 + lax.erf(v))
 
 
 def parts_of(A, H, channels):
@@ -321,7 +322,7 @@
     mx[CIN + 1:CIN + 2, :C1] = bo_ref[...]
     lift8 = jnp.concatenate([mx[0:8, :C1]], axis=0)
     columns = mx[...].T[:C1]
-    bo_col = columns[:, CIN + 1:CIN + 2]
+    bo_col = columns[:, CIN + 1:CIN + 2] * ROOT
 
     def left16(matrix, bias):
         n = matrix.shape[1]
@@ -341,7 +342,7 @@
     highest = lax.Precision.HIGHEST
     eighth = lax.broadcasted_iota(jnp.int32, (1, ones.shape[1]), 1) // 8
     m = jnp.dot(lift8, byp_ref[...], precision=highest, preferred_element_type=F32)
-    bp16 = left16(m, m[CIN:CIN + 1] + bi_ref[...])
+    bp16 = left16(m * ROOT, (m[CIN:CIN + 1] + bi_ref[...]) * ROOT)
     m = lax.dot_general(
         lift8, pr_ref[...], (((1,), (1,)), ((), ())), precision=highest, preferred_element_type=F32
     )
@@ -361,8 +362,8 @@
     bq_bd = diagonal(bpq[a * S + part], min(G1, 16)).astype(BF16)
     bp_bd = diagonal(bp_all, GROUP).astype(BF16)
     pl_bd = diagonal(pl16.astype(F32), FINE).astype(BF16)
-    wo_bd = wide(split(diagonal(wo_ref[...], GROUP)))
-    pr_bd = split(diagonal(pr_ref[...], FINE))
+    wo_bd = wide(split(diagonal(wo_ref[...] * 0.5, GROUP)))
+    pr_bd = split(diagonal(pr_ref[...] * ROOT, FINE))
     Q = J * KZ
     lifts = tall(split(lift8))
     for j in range(J):
@@ -468,7 +469,7 @@
             mul(bq_bd, jnp.concatenate([pk_ref[s * G1 + g + xx] for xx in range(count)], axis=0))
             for g in range(0, G1, count)
         ], axis=0)
-        g = split(gelu(v + near))
+        g = split(bend(v + near))
         zc[s] = wave(g)
         return carry
 
@@ -569,10 +570,10 @@
     def narrow_step(s, carry):
         v = mul(tall(split(vn[s])), tzi_ref[...])
         near = jnp.concatenate([pk_ref[part * HX + a * hx + s * GROUP + xx] for xx in range(GROUP)], axis=0)
-        g = split(gelu(v + mul(bp_bd, near)))
+        g = split(bend(v + mul(bp_bd, near)))
         narrow = mul(wo_bd, deep(g))
         for xx in range(GROUP):
-            nar[s * GROUP + xx] = narrow[xx * C1:(xx + 1) * C1]
+            nar[s * GROUP + xx] = narrow[xx * C1:(xx + 1) * C1] + bo_col
         return carry
 
     lax.fori_loop(0, hx // GROUP, narrow_step, 0)
@@ -624,8 +625,8 @@
                 for yy in range(YB):
                     at_y = (ch * YB + yy) // 2 * zn
                     pieces.append(half[:, at_y:at_y + zn])
-                rows += [jnp.concatenate(pieces, axis=1) + bo_col] * 2
-            g = split(gelu(v + jnp.concatenate(rows, axis=0)))
+                rows += [jnp.concatenate(pieces, axis=1)] * 2
+            g = split(bend(v + jnp.concatenate(rows, axis=0)))
             cols = slice(ch * width, (ch + 1) * width)
             res = left3(pr_bd, g) + mul(pl_bd, near[:, cols])
             for yy in range(YB):
@@ -675,7 +676,7 @@
 
     tz = z_table(zc)
     tzf = np.concatenate(list(halves(tz)), axis=1)
-    tzi = stacked(np.ascontiguousarray(tz.T) * back)
+    tzi = stacked(np.ascontiguousarray(tz.T) * (back * ROOT))
     fine_x = x_angles(A, xc, NX)
     half_x = x_angles(A, xc // 2, NX // 2)
     eye = np.eye(cin)
@@ -717,7 +718,7 @@
     V = pltpu.VMEM
     return pl.pallas_call(
         functools.partial(
-            kernel, A, B, xc, yc, 1.0 / math.sqrt(cells), 1.0 / math.sqrt(cells / 4.0), math.sqrt(cells)
+            kernel, A, B, xc, yc, 1.0 / math.sqrt(cells), ROOT / math.sqrt(cells / 4.0), math.sqrt(cells)
         ),
         out_shape=pltpu.VMEM((cin, xc, yc, zc), F32),
         in_specs=[anywhere] * len(operands),
@@ -738,7 +739,7 @@
             V((N, CQ, LB), F32), V((N, CQ, LB), F32), V((N, C1, LB), F32),
             V((xc // FINE, 2, FINE * C1, LB), F32),
             V((hx, C1, width), F32), V((xc, 16, yc * zc), BF16), V((16, yc * zc), F32),
-            V((GROUP * C2, GROUP * C2), F32), V((A * S, CQ, 16), F32),
+            V((GROUP * C2, max(GROUP * C2, FINE * C1)), F32), V((A * S, CQ, 16), F32),
             pltpu.SemaphoreType.DMA((cin,)),
             pltpu.SemaphoreType.DMA((18 + 2 * S,)),
             pltpu.SemaphoreType.DMA((10 + S,)), pltpu.SemaphoreType.DMA((10 + S + A * B // 2 + A * S // 2,)),

time: 40.5 us -> 40.1 us (level)
  Pallas kernels: 39.6 us -> 39.1 us
    pallas_call x1, Pallas kernels: 39.6 us -> 39.1 us  [on_device(): pl.pallas_call(functools.partial(kernel, A, B, xc, yc, 1.0 / math.sqrt(ce...]
where the time goes in v6:
time: 40.1 us; the launch traced here: 40 us
  Pallas kernels  39.1 us (98%)
  local copies, waits for them, and re-layouts  0.8 us (2%)
    pallas_call x1, Pallas kernels, on_device(): pl.pallas_call(functools.partial(kernel, A, B, xc, yc, 1.0 / math.sqrt(ce...  39.1 us

profile of v6, /device:TPU:0, one launch (start us, length us, event | category | flops | bytes accessed | tf_op | source)
XLA Modules:
  0.0 40.0 jit_solution(11246514097597942850)
XLA Ops:
  0.0 39.1 %shard_map.199 = f32[4,16,16,128]{3,2,1,0:T(8,128)S(1)} custom-call(f32[4,16,16,128]{3,2,1,0:T(8,128)} %f_hbm.1, f32[4,32]{1,0:T(4,128)} %bitcast.9, f32[1,32]{1,0:T(1,128)} %bitcast.10, f32[32,64]{1,0:T(8,128)} %bitcast.8, f32[1,64]{1,0:T(1,128)} %bitcast.11, f32[32,64]{1,0:T(8,128)} %wo_hbm.1, f32[1,32]{1,0:T(1,128)} %bitcast.12, f32[4,32]{1,0:T(4,128)} %pr_hbm.1, ...), custom_call_target="tpu_custom_call" | custom-call | tf_op jit(solution)/shard_map/pallas_call | solution.py:719
  39.2 0.8 %copy.23 = f32[4,16,16,128]{3,2,1,0:T(8,128)} copy(f32[4,16,16,128]{3,2,1,0:T(8,128)S(1)} %shard_map.199) | data formatting | bytes 1048576

commit v7 on v6

--- a/solution.py
+++ b/solution.py
@@ -482,7 +482,7 @@
             for ip in range(S):
                 fill_pooled(ia, ip)
     l_tzi.wait()
-    lax.fori_loop(0, S * steps, coarse_step, 0)
+    lax.fori_loop(0, S * steps, coarse_step, 0, unroll=True)
 
     l_xf.wait()
     for load in loads[18 + S:]:
@@ -554,6 +554,10 @@
     for t in range(B - 1, 0, -1):
         remote(ag2.at[me], ag2.at[me], EXP2, SPREAD + t, (a, flip(t)))
     spread(0)
+    for t in range(1, B):
+        source = a * B + flip(t)
+        arrive(ag2.at[source], SPREAD + t)
+        spread(t)
     for turn in range(S):
         near_finish(yall, LINE, turn)
     parts = []
@@ -576,12 +580,8 @@
             nar[s * GROUP + xx] = narrow[xx * C1:(xx + 1) * C1] + bo_col
         return carry
 
-    lax.fori_loop(0, hx // GROUP, narrow_step, 0)
-
-    for t in range(1, B):
-        source = a * B + flip(t)
-        arrive(ag2.at[source], SPREAD + t)
-        spread(t)
+    lax.fori_loop(0, hx // GROUP, narrow_step, 0, unroll=True)
+
     def expand(ia):
         rows = jnp.concatenate([
             jnp.concatenate([ag2[(ia * IL + g) * H + h] for h in range(H)], axis=1) for g in range(IL)

time: 40.1 us -> 39.4 us (0.983)
  Pallas kernels: 39.1 us -> 38.5 us
    pallas_call x1, Pallas kernels: 39.1 us -> 38.5 us  [on_device(): pl.pallas_call(functools.partial(kernel, A, B, xc, yc, 1.0 / math.sqrt(ce...]
where the time goes in v7:
time: 39.4 us; the launch traced here: 39.3 us
  Pallas kernels  38.5 us (98%)
  local copies, waits for them, and re-layouts  0.8 us (2%)
    pallas_call x1, Pallas kernels, on_device(): pl.pallas_call(functools.partial(kernel, A, B, xc, yc, 1.0 / math.sqrt(ce...  38.5 us
    unnamed x1, local copies, waits for them, and re-layouts  0.8 us

profile of v7, /device:TPU:0, one launch (start us, length us, event | category | flops | bytes accessed | tf_op | source)
XLA Modules:
  0.0 39.3 jit_solution(16817557100748559145)
XLA Ops:
  0.0 38.5 %shard_map.199 = f32[4,16,16,128]{3,2,1,0:T(8,128)S(1)} custom-call(f32[4,16,16,128]{3,2,1,0:T(8,128)} %f_hbm.1, f32[4,32]{1,0:T(4,128)} %bitcast.9, f32[1,32]{1,0:T(1,128)} %bitcast.10, f32[32,64]{1,0:T(8,128)} %bitcast.8, f32[1,64]{1,0:T(1,128)} %bitcast.11, f32[32,64]{1,0:T(8,128)} %wo_hbm.1, f32[1,32]{1,0:T(1,128)} %bitcast.12, f32[4,32]{1,0:T(4,128)} %pr_hbm.1, ...), custom_call_target="tpu_custom_call" | custom-call | tf_op jit(solution)/shard_map/pallas_call | solution.py:719
  38.5 0.8 %copy.23 = f32[4,16,16,128]{3,2,1,0:T(8,128)} copy(f32[4,16,16,128]{3,2,1,0:T(8,128)S(1)} %shard_map.199) | data formatting | bytes 1048576

commit v8 on v7

--- a/solution.py
+++ b/solution.py
@@ -539,7 +539,7 @@
             mixed = jnp.where(lane == q, real, jnp.where(lane == Q + q, imag, mixed))
     ag2[me] = mixed
 
-    NEARBY = B // 2
+    NEARBY = 3 * B // 4
 
     def spread(t):
         source = a * B + flip(t)

time: 39.4 us -> 39.1 us (level)
  no operation moved by 1% of the time
where the time goes in v8:
time: 39.1 us; the launch traced here: 39 us
  Pallas kernels  38.2 us (98%)
  local copies, waits for them, and re-layouts  0.8 us (2%)
    pallas_call x1, Pallas kernels, on_device(): pl.pallas_call(functools.partial(kernel, A, B, xc, yc, 1.0 / math.sqrt(ce...  38.2 us
    unnamed x1, local copies, waits for them, and re-layouts  0.8 us

profile of v8, /device:TPU:0, one launch (start us, length us, event | category | flops | bytes accessed | tf_op | source)
XLA Modules:
  0.0 39.0 jit_solution(14375959760521476820)
XLA Ops:
  0.0 38.2 %shard_map.199 = f32[4,16,16,128]{3,2,1,0:T(8,128)S(1)} custom-call(f32[4,16,16,128]{3,2,1,0:T(8,128)} %f_hbm.1, f32[4,32]{1,0:T(4,128)} %bitcast.9, f32[1,32]{1,0:T(1,128)} %bitcast.10, f32[32,64]{1,0:T(8,128)} %bitcast.8, f32[1,64]{1,0:T(1,128)} %bitcast.11, f32[32,64]{1,0:T(8,128)} %wo_hbm.1, f32[1,32]{1,0:T(1,128)} %bitcast.12, f32[4,32]{1,0:T(4,128)} %pr_hbm.1, ...), custom_call_target="tpu_custom_call" | custom-call | tf_op jit(solution)/shard_map/pallas_call | solution.py:719
  38.2 0.8 %copy.23 = f32[4,16,16,128]{3,2,1,0:T(8,128)} copy(f32[4,16,16,128]{3,2,1,0:T(8,128)S(1)} %shard_map.199) | data formatting | bytes 1048576
